TPU v7x, 32 devices: a whole 2x2x4 slice. The times are simulated.
32 devices in a mesh: groups: 2 (over y), shots: 4 (over z), dom: 2 (over x), sub: 2 (over core).
Axes of the slice: x: 2, y: 2, z: 4, core: 2. Of those that a mesh axis runs over, the one named last changes fastest.
Arguments:
- velocity: float32 [64, 16, 256], P(('groups', 'shots'), 'dom', 'sub'), parts along dimension 0, may hold values from 0.15 to 0.4
- wave_prev: bfloat16 [8, 32, 16, 256], P(('groups', 'shots'), None, 'dom', 'sub'), parts along dimension 0, may hold values from -6 to 6
- wave_now: bfloat16 [8, 32, 16, 256], P(('groups', 'shots'), None, 'dom', 'sub'), parts along dimension 0, may hold values from -6 to 6
- adj_next: bfloat16 [8, 32, 16, 256], P(('groups', 'shots'), None, 'dom', 'sub'), parts along dimension 0, may hold values from -6 to 6
- adj_now: bfloat16 [8, 32, 16, 256], P(('groups', 'shots'), None, 'dom', 'sub'), parts along dimension 0, may hold values from -6 to 6
- sponge: int32 [32, 16, 256], P(None, 'dom', 'sub'), may hold values 0 or 1
- wavelet: float32 [8, 6], P(('groups', 'shots')), parts along dimension 0, may hold values from -12 to 12
- src_pos: int32 [8], P(('groups', 'shots')), parts along dimension 0, may hold values from 0 to 4095
- rec_pos: int32 [8, 256], P(('groups', 'shots')), parts along dimension 0, may hold values from 0 to 4095
- observed: float32 [8, 4, 256], P(('groups', 'shots')), parts along dimension 0, may hold values from -6 to 6
Outputs:
- direction: float32 [64, 16, 256], P(('groups', 'shots'), 'dom', 'sub'), parts along dimension 0
- wave_out: float32 [8, 32, 16, 256], P(('groups', 'shots'), None, 'dom', 'sub'), parts along dimension 0
There are 2 independent parts, one for each index of `groups`. A program takes and returns all parts, laid end to end along the dimension named above; an argument that names none is the same for every part. Nothing has to cross between parts.
Inputs may be any that keep to these rules, and one draw needn't show every extreme that they name: `src_pos`: a horizontal position x * 256 + y on the grid. `rec_pos`: horizontal positions x * 256 + y on the grid, possibly repeated.
All inputs are finite; a program needn't handle non-finite values. Where the computation divides by a largest or mean magnitude, that divisor is 1e-20 or more. No bound on the sum of `sponge` on one device may be relied on, other than what follows from the above.
Results may differ from a plain program's by a relative error of at most 0.0003.
Values sent between devices are 32-bit elements; how exact they have to be, the bound alone decides.
A program may use at most 64 MiB of HBM per device.

v0:
```python
import jax
import jax.numpy as jnp
from jax import lax
from jax.sharding import PartitionSpec as P

NF = 4
NFIN = 2
coeffs = (-205.0 / 72.0, 8.0 / 5.0, -1.0 / 5.0, 8.0 / 315.0, -1.0 / 560.0)
damp_rate = 0.2
step_rate = 0.1
floor_share = 0.5
src_depth = 2
rec_depth = 1
reach = 4


def padded_2(cells, sides, width):
    for axis, dim in sides:
        count = lax.axis_size(axis)
        ends = count - 1
        head = lax.slice_in_dim(cells, 0, width, axis=dim)
        tail = lax.slice_in_dim(cells, cells.shape[dim] - width, cells.shape[dim], axis=dim)
        cells = jnp.concatenate(
            [
                lax.ppermute(tail, axis, [(i, (i + 1) % count) for i in range(ends)]),
                cells,
                lax.ppermute(head, axis, [((i + 1) % count, i) for i in range(ends)]),
            ],
            axis=dim,
        )
    return cells


def laplace(padded, depth, rows, cols):
    z0, x0, y0 = (reach, reach, reach)
    total = 3.0 * coeffs[0] * padded[z0 : z0 + depth, x0 : x0 + rows, y0 : y0 + cols]
    for offset in range(1, 5):
        pair = padded[z0 + offset : z0 + offset + depth, x0 : x0 + rows, y0 : y0 + cols]
        pair = pair + padded[z0 - offset : z0 - offset + depth, x0 : x0 + rows, y0 : y0 + cols]
        pair = pair + padded[z0 : z0 + depth, x0 + offset : x0 + offset + rows, y0 : y0 + cols]
        pair = pair + padded[z0 : z0 + depth, x0 - offset : x0 - offset + rows, y0 : y0 + cols]
        pair = pair + padded[z0 : z0 + depth, x0 : x0 + rows, y0 + offset : y0 + offset + cols]
        pair = pair + padded[z0 : z0 + depth, x0 : x0 + rows, y0 - offset : y0 - offset + cols]
        total = total + coeffs[offset] * pair
    return total


def advance(now, before, kappa, damp, plane, level):
    widened = padded_2(now, (("dom", 1), ("sub", 2)), 4)
    padded = jnp.pad(widened, ((reach, reach), (0, 0), (0, 0)))
    lap = laplace(padded, now.shape[0], now.shape[1], now.shape[2])
    numer = 2.0 * now - (1.0 - damp) * before + kappa * lap
    numer = numer.at[level].add(plane)
    return numer / (1.0 + damp)


def local_spots(positions, rows, cols):
    cols_all = cols * lax.axis_size("sub")
    gx = positions // cols_all
    gy = positions % cols_all
    local_x = gx - lax.axis_index("dom") * rows
    local_y = gy - lax.axis_index("sub") * cols
    inside = (local_x >= 0) & (local_x < rows) & (local_y >= 0) & (local_y < cols)
    spots = jnp.where(inside, local_x * cols + local_y, 0)
    return (spots, inside)


def place_local(spots, inside, values, rows, cols):
    kept = jnp.where(inside, values, 0.0)
    flat = jnp.zeros((rows * cols,), jnp.float32).at[spots].add(kept)
    return flat.reshape(rows, cols)


def shards(
    velocity, wave_prev, wave_now, adj_next, adj_now, sponge, wavelet, src_pos, rec_pos, observed
):
    depth, rows, cols = sponge.shape
    full_vel = lax.all_gather(velocity, "shots", axis=0, tiled=True)
    kappa = full_vel * full_vel
    damp = damp_rate * sponge.astype(jnp.float32)
    amps = wavelet[0]
    src_spot, src_inside = local_spots(src_pos, rows, cols)
    rec_spot, rec_inside = local_spots(rec_pos[0], rows, cols)
    states = [wave_prev[0].astype(jnp.float32), wave_now[0].astype(jnp.float32)]
    for step in range(NF):
        plane = place_local(src_spot, src_inside, amps[step][None], rows, cols)
        states.append(advance(states[-1], states[-2], kappa, damp, plane, src_depth))
    lam_after = adj_next[0].astype(jnp.float32)
    lam_now = adj_now[0].astype(jnp.float32)
    grad = jnp.zeros_like(kappa)
    for level in range(NF, 0, -1):
        sampled = states[level + 1][rec_depth].reshape(-1)[rec_spot]
        resid = sampled - observed[0, level - 1]
        plane = place_local(rec_spot, rec_inside, resid, rows, cols)
        lam_before = advance(lam_now, lam_after, kappa, damp, plane, rec_depth)
        lower = level - 1
        accel = states[lower + 2] - 2.0 * states[lower + 1] + states[lower]
        grad = grad + lam_before * accel
        lam_after, lam_now = (lam_now, lam_before)
    illum = jnp.zeros_like(kappa)
    for level in range(1, NF + 1):
        illum = illum + states[level + 1] * states[level + 1]
    shot_count = lax.axis_size("shots")
    grad_all, illum_all = lax.psum((grad, illum), "shots")
    precond = grad_all / (illum_all + floor_share * shot_count)
    peak = lax.pmax(jnp.max(jnp.abs(precond)), ("dom", "sub"))
    full_dir = precond / (peak + 1e-06)
    updated = full_vel * (1.0 - step_rate * full_dir)
    owned = velocity.shape[0]
    direction = lax.dynamic_slice_in_dim(full_dir, lax.axis_index("shots") * owned, owned, 0)
    kappa_new = updated * updated
    before, current = (states[-2], states[-1])
    for step in range(NFIN):
        plane = place_local(src_spot, src_inside, amps[NF + step][None], rows, cols)
        following = advance(current, before, kappa_new, damp, plane, src_depth)
        before, current = (current, following)
    return (direction, current[None])


def solution(mesh):
    return jax.shard_map(
        shards,
        mesh=mesh,
        in_specs=(
            P(("groups", "shots"), "dom", "sub"),
            P(("groups", "shots"), None, "dom", "sub"),
            P(("groups", "shots"), None, "dom", "sub"),
            P(("groups", "shots"), None, "dom", "sub"),
            P(("groups", "shots"), None, "dom", "sub"),
            P(None, "dom", "sub"),
            P(("groups", "shots"), None),
            P(("groups", "shots")),
            P(("groups", "shots"), None),
            P(("groups", "shots"), None, None),
        ),
        out_specs=(
            P(("groups", "shots"), "dom", "sub"),
            P(("groups", "shots"), None, "dom", "sub"),
        ),
        check_vma=False,
    )
```

profile of v0, /device:TPU:0, one launch (start us, length us, event | category | flops | bytes accessed | tf_op | source)
XLA Modules:
  0.0 231.8 jit_solution(6835556315163786703)
XLA Ops:
  8.1 4.9 %collective-permute-start.4 = (f32[32,4,128]{2,1,0:T(4,128)S(1)}, f32[32,4,128]{2,1,0:T(4,128)S(1)}, u32[]{:S(2)}, u32[]{:S(2)}) collective-permute-start(f32[32,4,128]{2,1,0:T(4,128)S(1)} %get-tuple-element.261), channel_id=1, source_target_pairs={{0,2},{1,3},{4,6},{5,7},{8,10},{9,11},{12,14},{13,15},{16,18},{17,... | collective-permute-start | bytes 196616 | tf_op jit(solution)/shard_map/ppermute | solution.py:25
  13.0 1.3 collective-permute-start.5
  14.3 4.5 %collective-permute-start = (f32[32,4,128]{2,1,0:T(4,128)S(1)}, f32[32,4,128]{2,1,0:T(4,128)S(1)}, u32[]{:S(2)}, u32[]{:S(2)}) collective-permute-start(f32[32,4,128]{2,1,0:T(4,128)S(1)} %get-tuple-element.251), channel_id=1, source_target_pairs={{0,2},{1,3},{4,6},{5,7},{8,10},{9,11},{12,14},{13,15},{16,18},{17,... | collective-permute-start | bytes 196616 | tf_op jit(solution)/shard_map/ppermute | solution.py:25
  18.9 1.3 collective-permute-start.1
  27.0 2.6 %fusion.344 = f32[1024]{0:T(1024)S(1)} fusion(f32[1024]{0:T(1024)S(1)} %broadcast.395.clone, s32[]{:T(128)} %bitcast.12, pred[1]{0:T(512)(128)(4,1)} %get-tuple-element.275, f32[1,1]{1,0:T(1,128)} %get-tuple-element.270, s32[1]{0:T(128)} %compare_select_fusion.1), kind=kLoop, calls=%fused_computation.685 | loop fusion | flops 5 | bytes 525 | tf_op jit(solution)/shard_map/scatter-add | solution.py:70
  29.6 2.6 %fusion.342 = f32[1024]{0:T(1024)S(1)} fusion(f32[1024]{0:T(1024)S(1)} %broadcast.395.clone.1, s32[]{:T(128)} %bitcast.12, pred[1]{0:T(512)(128)(4,1)} %get-tuple-element.275, f32[1,1]{1,0:T(1,128)} %get-tuple-element.269, s32[1]{0:T(128)} %compare_select_fusion.1), kind=kLoop, calls=%fused_computation.682 | loop fusion | flops 5 | bytes 525 | tf_op jit(solution)/shard_map/scatter-add | solution.py:70
  32.3 2.6 %fusion.340 = f32[1024]{0:T(1024)S(1)} fusion(f32[1024]{0:T(1024)S(1)} %broadcast.395.clone.2, s32[]{:T(128)} %bitcast.12, pred[1]{0:T(512)(128)(4,1)} %get-tuple-element.275, f32[1,1]{1,0:T(1,128)} %get-tuple-element.268, s32[1]{0:T(128)} %compare_select_fusion.1), kind=kLoop, calls=%fused_computation.679 | loop fusion | flops 5 | bytes 525 | tf_op jit(solution)/shard_map/scatter-add | solution.py:70
  34.9 2.6 %fusion.338 = f32[1024]{0:T(1024)S(1)} fusion(f32[1024]{0:T(1024)S(1)} %broadcast.395.clone.3, s32[]{:T(128)} %bitcast.12, pred[1]{0:T(512)(128)(4,1)} %get-tuple-element.275, f32[1,1]{1,0:T(1,128)} %get-tuple-element.267, s32[1]{0:T(128)} %compare_select_fusion.1), kind=kLoop, calls=%fused_computation.676 | loop fusion | flops 5 | bytes 525 | tf_op jit(solution)/shard_map/scatter-add | solution.py:70
  37.5 13.6 %all_gather.3 = f32[32,8,128]{2,1,0:T(8,128)S(1)} all-gather(f32[8,8,128]{2,1,0:T(8,128)S(1)} %copy-done.7), channel_id=1, replica_groups=mesh['groups'=2,'shots'=4,'dom'=2,'sub'=2] {'shots'}, dimensions={0}, use_global_device_ids=true | all-gather | bytes 163840 | tf_op jit(solution)/shard_map/all_gather | solution.py:78
  51.3 1.3 collective-permute-start.6
  52.6 1.3 collective-permute-start.7
  54.1 3.1 %collective-permute-start.2 = (f32[32,16,4]{2,1,0:T(8,128)S(1)}, f32[32,16,4]{2,1,0:T(8,128)S(1)}, u32[]{:S(2)}, u32[]{:S(2)}) collective-permute-start(f32[32,16,4]{2,1,0:T(8,128)S(1)} %get-tuple-element.221), channel_id=1, source_target_pairs={{0,1},{2,3},{4,5},{6,7},{8,9},{10,11},{12,13},{14,15},{16,17},{18,... | collective-permute-start | bytes 24584 | tf_op jit(solution)/shard_map/ppermute | solution.py:25
  57.2 1.3 collective-permute-start.3
  60.5 4.5 %collective-permute-start.8 = (f32[32,4,128]{2,1,0:T(4,128)S(1)}, f32[32,4,128]{2,1,0:T(4,128)S(1)}, u32[]{:S(2)}, u32[]{:S(2)}) collective-permute-start(f32[32,4,128]{2,1,0:T(4,128)S(1)} %get-tuple-element.259), channel_id=1, source_target_pairs={{0,2},{1,3},{4,6},{5,7},{8,10},{9,11},{12,14},{13,15},{16,18},{17,... | collective-permute-start | bytes 196616 | tf_op jit(solution)/shard_map/ppermute | solution.py:25
  65.0 1.3 collective-permute-start.9
  67.3 4.5 %collective-permute-done.9 = f32[32,4,128]{2,1,0:T(4,128)S(1)} collective-permute-done((f32[32,4,128]{2,1,0:T(4,128)S(1)}, f32[32,4,128]{2,1,0:T(4,128)S(1)}, u32[]{:S(2)}, u32[]{:S(2)}) %collective-permute-start.9) | collective-permute-done | bytes 65568 | tf_op jit(solution)/shard_map/ppermute | solution.py:27
  72.0 1.9 collective-permute-start.10
  73.9 1.3 collective-permute-start.11
  75.9 1.5 collective-permute-done.11
  78.8 1.5 collective-permute-start.12
  80.3 1.3 collective-permute-start.13
  81.6 1.4 gather_fusion.3
  83.0 3.5 %collective-permute-done.13 = f32[32,4,128]{2,1,0:T(4,128)S(1)} collective-permute-done((f32[32,4,128]{2,1,0:T(4,128)S(1)}, f32[32,4,128]{2,1,0:T(4,128)S(1)}, u32[]{:S(2)}, u32[]{:S(2)}) %collective-permute-start.13) | collective-permute-done | bytes 65568 | tf_op jit(solution)/shard_map/ppermute | solution.py:27
  86.6 1.3 collective-permute-start.14
  87.9 1.3 collective-permute-start.15
  89.3 2.1 collective-permute-done.15
  92.8 1.6 collective-permute-start.16
  94.4 1.3 collective-permute-start.17
  95.7 1.4 gather_fusion.2
  97.1 3.5 %collective-permute-done.17 = f32[32,4,128]{2,1,0:T(4,128)S(1)} collective-permute-done((f32[32,4,128]{2,1,0:T(4,128)S(1)}, f32[32,4,128]{2,1,0:T(4,128)S(1)}, u32[]{:S(2)}, u32[]{:S(2)}) %collective-permute-start.17) | collective-permute-done | bytes 65568 | tf_op jit(solution)/shard_map/ppermute | solution.py:27
  100.8 1.3 collective-permute-start.18
  102.1 1.5 collective-permute-start.19
  103.6 1.4 gather_fusion.1
  107.6 1.4 gather_fusion
  109.0 2.3 %scatter_custom_fusion = f32[1024]{0:T(1024)S(1)} fusion(s32[256]{0:T(256)S(1)} %bitcast.109, f32[256]{0:T(256)S(1)} %get-tuple-element.274, f32[]{:T(128)} %constant.405.clone.1), kind=kCustom, calls=%fused_computation.646 | custom fusion | flops 256 | bytes 4100 | tf_op jit(solution)/shard_map/scatter-add | solution.py:70
  111.4 1.6 collective-permute-start.20
  113.0 1.3 collective-permute-start.21
  115.1 4.1 %collective-permute-done.21 = f32[32,4,128]{2,1,0:T(4,128)S(1)} collective-permute-done((f32[32,4,128]{2,1,0:T(4,128)S(1)}, f32[32,4,128]{2,1,0:T(4,128)S(1)}, u32[]{:S(2)}, u32[]{:S(2)}) %collective-permute-start.21) | collective-permute-done | bytes 65568 | tf_op jit(solution)/shard_map/ppermute | solution.py:27
  119.4 1.4 collective-permute-start.22
  120.8 1.3 collective-permute-start.23
  122.1 2.3 %scatter_custom_fusion.1 = f32[1024]{0:T(1024)S(1)} fusion(s32[256]{0:T(256)S(1)} %bitcast.110, f32[256]{0:T(256)S(1)} %get-tuple-element.273, f32[]{:T(128)} %constant.405.clone.1), kind=kCustom, calls=%fused_computation.644 | custom fusion | flops 256 | bytes 4100 | tf_op jit(solution)/shard_map/scatter-add | solution.py:70
  125.9 1.5 collective-permute-start.24
  127.4 1.3 collective-permute-start.25
  129.7 4.5 %collective-permute-done.25 = f32[32,4,128]{2,1,0:T(4,128)S(1)} collective-permute-done((f32[32,4,128]{2,1,0:T(4,128)S(1)}, f32[32,4,128]{2,1,0:T(4,128)S(1)}, u32[]{:S(2)}, u32[]{:S(2)}) %collective-permute-start.25) | collective-permute-done | bytes 65568 | tf_op jit(solution)/shard_map/ppermute | solution.py:27
  134.4 2.0 collective-permute-start.26
  136.4 1.3 collective-permute-start.27
  137.7 2.3 %scatter_custom_fusion.3 = f32[1024]{0:T(1024)S(1)} fusion(s32[256]{0:T(256)S(1)} %bitcast.111, f32[256]{0:T(256)S(1)} %get-tuple-element.200, f32[]{:T(128)} %constant.405.clone.1), kind=kCustom, calls=%fused_computation.640 | custom fusion | flops 256 | bytes 4100 | tf_op jit(solution)/shard_map/scatter-add | solution.py:70
  140.0 2.3 %scatter_custom_fusion.2 = f32[1024]{0:T(1024)S(1)} fusion(s32[256]{0:T(256)S(1)} %bitcast.112, f32[256]{0:T(256)S(1)} %get-tuple-element.272, f32[]{:T(128)} %constant.405.clone.1), kind=kCustom, calls=%fused_computation.642 | custom fusion | flops 256 | bytes 4100 | tf_op jit(solution)/shard_map/scatter-add | solution.py:70
  143.8 1.5 collective-permute-start.28
  145.3 1.3 collective-permute-start.29
  146.6 4.5 %collective-permute-start.32 = (f32[32,4,128]{2,1,0:T(4,128)S(1)}, f32[32,4,128]{2,1,0:T(4,128)S(1)}, u32[]{:S(2)}, u32[]{:S(2)}) collective-permute-start(f32[32,4,128]{2,1,0:T(4,128)S(1)} %get-tuple-element.253), channel_id=1, source_target_pairs={{0,2},{1,3},{4,6},{5,7},{8,10},{9,11},{12,14},{13,15},{16,18},{17,... | collective-permute-start | bytes 196616 | tf_op jit(solution)/shard_map/ppermute | solution.py:25
  151.2 1.3 collective-permute-start.33
  152.7 2.3 %collective-permute-start.30 = (f32[32,16,4]{2,1,0:T(8,128)S(1)}, f32[32,16,4]{2,1,0:T(8,128)S(1)}, u32[]{:S(2)}, u32[]{:S(2)}) collective-permute-start(f32[32,16,4]{2,1,0:T(8,128)S(1)} %get-tuple-element.209), channel_id=1, source_target_pairs={{0,1},{2,3},{4,5},{6,7},{8,9},{10,11},{12,13},{14,15},{16,17},{18,... | collective-permute-start | bytes 24584 | tf_op jit(solution)/shard_map/ppermute | solution.py:25
  155.0 1.5 collective-permute-start.31
  160.8 2.1 collective-permute-start.34
  164.2 2.6 %fusion.336 = f32[1024]{0:T(1024)S(1)} fusion(f32[1024]{0:T(1024)S(1)} %broadcast.395.clone.4, s32[]{:T(128)} %bitcast.12, pred[1]{0:T(512)(128)(4,1)} %get-tuple-element.275, f32[1,1]{1,0:T(1,128)} %get-tuple-element.271, s32[1]{0:T(128)} %compare_select_fusion.1), kind=kLoop, calls=%fused_computation.673 | loop fusion | flops 5 | bytes 525 | tf_op jit(solution)/shard_map/scatter-add | solution.py:70
  167.1 31.3 %all-reduce.13.cloned.1.call-done = (f32[32,8,128]{2,1,0:T(8,128)}, f32[32,8,128]{2,1,0:T(8,128)}) async-done(((f32[32,8,128]{2,1,0:T(8,128)}, f32[32,8,128]{2,1,0:T(8,128)}), (f32[32,8,128]{2,1,0:T(8,128)}, f32[32,8,128]{2,1,0:T(8,128)})) %all-reduce.13.cloned.1.call-update) | async-done | bytes 262160 | tf_op jit(solution)/shard_map/psum | solution.py:104
  198.4 1.6 abs_reduce_fusion
  200.4 6.3 %pmax.7 = f32[]{:T(128)} all-reduce(f32[]{:T(128)} %abs_reduce_fusion), channel_id=1, replica_groups=mesh['groups'=2,'shots'=4,'dom'=2,'sub'=2] {'dom','sub'}, use_global_device_ids=true, to_apply=%region_7.8 | all-reduce | flops 1 | bytes 8 | tf_op jit(solution)/shard_map/pmax | solution.py:106
  208.1 3.6 %collective-permute-start.36 = (f32[32,4,128]{2,1,0:T(4,128)S(1)}, f32[32,4,128]{2,1,0:T(4,128)S(1)}, u32[]{:S(2)}, u32[]{:S(2)}) collective-permute-start(f32[32,4,128]{2,1,0:T(4,128)S(1)} %get-tuple-element.243), channel_id=1, source_target_pairs={{0,2},{1,3},{4,6},{5,7},{8,10},{9,11},{12,14},{13,15},{16,18},{17,... | collective-permute-start | bytes 196616 | tf_op jit(solution)/shard_map/ppermute | solution.py:25
  213.1 2.6 %fusion.334 = f32[1024]{0:T(1024)S(1)} fusion(f32[1024]{0:T(1024)S(1)} %broadcast.395.clone.5, s32[]{:T(128)} %bitcast.12, pred[1]{0:T(512)(128)(4,1)} %get-tuple-element.275, f32[1,1]{1,0:T(1,128)} %get-tuple-element.266, s32[1]{0:T(128)} %compare_select_fusion.1), kind=kLoop, calls=%fused_computation.670 | loop fusion | flops 5 | bytes 525 | tf_op jit(solution)/shard_map/scatter-add | solution.py:70
  215.7 2.2 collective-permute-done.37
  218.1 1.3 collective-permute-start.38
  221.3 1.5 collective-permute-done.39
  (158 shorter events, 31.8 us)
Async XLA Ops:
  7.2 191.2 %all-reduce.13.cloned.1.call-start = ((), (), s32[]{:S(2)}) async-start(), calls=%async_computation | async-start | bytes 524288 | tf_op jit(solution)/shard_map/psum | solution.py:104
  8.1 6.2 %copy-start.4 = (bf16[1,32,8,128]{3,2,1,0:T(8,128)(2,1)S(1)}, bf16[1,32,8,128]{3,2,1,0:T(8,128)(2,1)}, u32[]{:S(2)}) copy-start(bf16[1,32,8,128]{3,2,1,0:T(8,128)(2,1)} %param.46) | copy-start | bytes 196612
  8.1 43.0 %collective-permute-start.4 = (f32[32,4,128]{2,1,0:T(4,128)S(1)}, f32[32,4,128]{2,1,0:T(4,128)S(1)}, u32[]{:S(2)}, u32[]{:S(2)}) collective-permute-start(f32[32,4,128]{2,1,0:T(4,128)S(1)} %get-tuple-element.261), channel_id=1, source_target_pairs={{0,2},{1,3},{4,6},{5,7},{8,10},{9,11},{12,14},{13,15},{16,18},{17,... | collective-permute-start | bytes 196616 | tf_op jit(solution)/shard_map/ppermute | solution.py:25
  13.0 38.1 %collective-permute-start.5 = (f32[32,4,128]{2,1,0:T(4,128)S(1)}, f32[32,4,128]{2,1,0:T(4,128)S(1)}, u32[]{:S(2)}, u32[]{:S(2)}) collective-permute-start(f32[32,4,128]{2,1,0:T(4,128)S(1)} %get-tuple-element.260), channel_id=1, source_target_pairs={{2,0},{3,1},{6,4},{7,5},{10,8},{11,9},{14,12},{15,13},{18,16},{19,... | collective-permute-start | bytes 196616 | tf_op jit(solution)/shard_map/ppermute | solution.py:27
  14.3 39.5 %collective-permute-start = (f32[32,4,128]{2,1,0:T(4,128)S(1)}, f32[32,4,128]{2,1,0:T(4,128)S(1)}, u32[]{:S(2)}, u32[]{:S(2)}) collective-permute-start(f32[32,4,128]{2,1,0:T(4,128)S(1)} %get-tuple-element.251), channel_id=1, source_target_pairs={{0,2},{1,3},{4,6},{5,7},{8,10},{9,11},{12,14},{13,15},{16,18},{17,... | collective-permute-start | bytes 196616 | tf_op jit(solution)/shard_map/ppermute | solution.py:25
  18.9 35.0 %collective-permute-start.1 = (f32[32,4,128]{2,1,0:T(4,128)S(1)}, f32[32,4,128]{2,1,0:T(4,128)S(1)}, u32[]{:S(2)}, u32[]{:S(2)}) collective-permute-start(f32[32,4,128]{2,1,0:T(4,128)S(1)} %get-tuple-element.250), channel_id=1, source_target_pairs={{2,0},{3,1},{6,4},{7,5},{10,8},{11,9},{14,12},{15,13},{18,16},{19,... | collective-permute-start | bytes 196616 | tf_op jit(solution)/shard_map/ppermute | solution.py:27
  20.2 0.7 copy-start.8
  20.2 1.3 copy-start.9
  21.5 0.7 copy-start.10
  22.2 15.3 %copy-start.7 = (f32[8,8,128]{2,1,0:T(8,128)S(1)}, f32[8,8,128]{2,1,0:T(8,128)}, u32[]{:S(2)}) copy-start(f32[8,8,128]{2,1,0:T(8,128)} %param.42) | copy-start | bytes 98308
  51.3 7.2 %collective-permute-start.6 = (f32[32,16,4]{2,1,0:T(8,128)S(1)}, f32[32,16,4]{2,1,0:T(8,128)S(1)}, u32[]{:S(2)}, u32[]{:S(2)}) collective-permute-start(f32[32,16,4]{2,1,0:T(8,128)S(1)} %get-tuple-element.241), channel_id=1, source_target_pairs={{0,1},{2,3},{4,5},{6,7},{8,9},{10,11},{12,13},{14,15},{16,17},{18,... | collective-permute-start | bytes 24584 | tf_op jit(solution)/shard_map/ppermute | solution.py:25
  52.6 5.9 %collective-permute-start.7 = (f32[32,16,4]{2,1,0:T(8,128)S(1)}, f32[32,16,4]{2,1,0:T(8,128)S(1)}, u32[]{:S(2)}, u32[]{:S(2)}) collective-permute-start(f32[32,16,4]{2,1,0:T(8,128)S(1)} %get-tuple-element.240), channel_id=1, source_target_pairs={{1,0},{3,2},{5,4},{7,6},{9,8},{11,10},{13,12},{15,14},{17,16},{19,... | collective-permute-start | bytes 24584 | tf_op jit(solution)/shard_map/ppermute | solution.py:27
  54.1 12.2 %collective-permute-start.2 = (f32[32,16,4]{2,1,0:T(8,128)S(1)}, f32[32,16,4]{2,1,0:T(8,128)S(1)}, u32[]{:S(2)}, u32[]{:S(2)}) collective-permute-start(f32[32,16,4]{2,1,0:T(8,128)S(1)} %get-tuple-element.221), channel_id=1, source_target_pairs={{0,1},{2,3},{4,5},{6,7},{8,9},{10,11},{12,13},{14,15},{16,17},{18,... | collective-permute-start | bytes 24584 | tf_op jit(solution)/shard_map/ppermute | solution.py:25
  57.2 9.2 %collective-permute-start.3 = (f32[32,16,4]{2,1,0:T(8,128)S(1)}, f32[32,16,4]{2,1,0:T(8,128)S(1)}, u32[]{:S(2)}, u32[]{:S(2)}) collective-permute-start(f32[32,16,4]{2,1,0:T(8,128)S(1)} %get-tuple-element.220), channel_id=1, source_target_pairs={{1,0},{3,2},{5,4},{7,6},{9,8},{11,10},{13,12},{15,14},{17,16},{19,... | collective-permute-start | bytes 24584 | tf_op jit(solution)/shard_map/ppermute | solution.py:27
  58.8 0.9 copy-start
  58.9 0.9 copy-start.1
  58.9 0.9 copy-start.5
  60.5 6.9 %collective-permute-start.8 = (f32[32,4,128]{2,1,0:T(4,128)S(1)}, f32[32,4,128]{2,1,0:T(4,128)S(1)}, u32[]{:S(2)}, u32[]{:S(2)}) collective-permute-start(f32[32,4,128]{2,1,0:T(4,128)S(1)} %get-tuple-element.259), channel_id=1, source_target_pairs={{0,2},{1,3},{4,6},{5,7},{8,10},{9,11},{12,14},{13,15},{16,18},{17,... | collective-permute-start | bytes 196616 | tf_op jit(solution)/shard_map/ppermute | solution.py:25
  65.0 6.7 %collective-permute-start.9 = (f32[32,4,128]{2,1,0:T(4,128)S(1)}, f32[32,4,128]{2,1,0:T(4,128)S(1)}, u32[]{:S(2)}, u32[]{:S(2)}) collective-permute-start(f32[32,4,128]{2,1,0:T(4,128)S(1)} %get-tuple-element.258), channel_id=1, source_target_pairs={{2,0},{3,1},{6,4},{7,5},{10,8},{11,9},{14,12},{15,13},{18,16},{19,... | collective-permute-start | bytes 196616 | tf_op jit(solution)/shard_map/ppermute | solution.py:27
  71.8 3.4 %copy-start.6 = (bf16[1,32,8,128]{3,2,1,0:T(8,128)(2,1)S(1)}, bf16[1,32,8,128]{3,2,1,0:T(8,128)(2,1)}, u32[]{:S(2)}) copy-start(bf16[1,32,8,128]{3,2,1,0:T(8,128)(2,1)} %param.45) | copy-start | bytes 196612
  72.0 3.9 %collective-permute-start.10 = (f32[32,16,4]{2,1,0:T(8,128)S(1)}, f32[32,16,4]{2,1,0:T(8,128)S(1)}, u32[]{:S(2)}, u32[]{:S(2)}) collective-permute-start(f32[32,16,4]{2,1,0:T(8,128)S(1)} %get-tuple-element.237), channel_id=1, source_target_pairs={{0,1},{2,3},{4,5},{6,7},{8,9},{10,11},{12,13},{14,15},{16,17},{18,... | collective-permute-start | bytes 24584 | tf_op jit(solution)/shard_map/ppermute | solution.py:25
  73.9 3.4 %collective-permute-start.11 = (f32[32,16,4]{2,1,0:T(8,128)S(1)}, f32[32,16,4]{2,1,0:T(8,128)S(1)}, u32[]{:S(2)}, u32[]{:S(2)}) collective-permute-start(f32[32,16,4]{2,1,0:T(8,128)S(1)} %get-tuple-element.236), channel_id=1, source_target_pairs={{1,0},{3,2},{5,4},{7,6},{9,8},{11,10},{13,12},{15,14},{17,16},{19,... | collective-permute-start | bytes 24584 | tf_op jit(solution)/shard_map/ppermute | solution.py:27
  78.8 4.1 %collective-permute-start.12 = (f32[32,4,128]{2,1,0:T(4,128)S(1)}, f32[32,4,128]{2,1,0:T(4,128)S(1)}, u32[]{:S(2)}, u32[]{:S(2)}) collective-permute-start(f32[32,4,128]{2,1,0:T(4,128)S(1)} %get-tuple-element.257), channel_id=1, source_target_pairs={{0,2},{1,3},{4,6},{5,7},{8,10},{9,11},{12,14},{13,15},{16,18},{17,... | collective-permute-start | bytes 196616 | tf_op jit(solution)/shard_map/ppermute | solution.py:25
  80.3 6.2 %collective-permute-start.13 = (f32[32,4,128]{2,1,0:T(4,128)S(1)}, f32[32,4,128]{2,1,0:T(4,128)S(1)}, u32[]{:S(2)}, u32[]{:S(2)}) collective-permute-start(f32[32,4,128]{2,1,0:T(4,128)S(1)} %get-tuple-element.256), channel_id=1, source_target_pairs={{2,0},{3,1},{6,4},{7,5},{10,8},{11,9},{14,12},{15,13},{18,16},{19,... | collective-permute-start | bytes 196616 | tf_op jit(solution)/shard_map/ppermute | solution.py:27
  86.6 2.6 %collective-permute-start.14 = (f32[32,16,4]{2,1,0:T(8,128)S(1)}, f32[32,16,4]{2,1,0:T(8,128)S(1)}, u32[]{:S(2)}, u32[]{:S(2)}) collective-permute-start(f32[32,16,4]{2,1,0:T(8,128)S(1)} %get-tuple-element.233), channel_id=1, source_target_pairs={{0,1},{2,3},{4,5},{6,7},{8,9},{10,11},{12,13},{14,15},{16,17},{18,... | collective-permute-start | bytes 24584 | tf_op jit(solution)/shard_map/ppermute | solution.py:25
  87.9 3.4 %collective-permute-start.15 = (f32[32,16,4]{2,1,0:T(8,128)S(1)}, f32[32,16,4]{2,1,0:T(8,128)S(1)}, u32[]{:S(2)}, u32[]{:S(2)}) collective-permute-start(f32[32,16,4]{2,1,0:T(8,128)S(1)} %get-tuple-element.232), channel_id=1, source_target_pairs={{1,0},{3,2},{5,4},{7,6},{9,8},{11,10},{13,12},{15,14},{17,16},{19,... | collective-permute-start | bytes 24584 | tf_op jit(solution)/shard_map/ppermute | solution.py:27
  92.8 4.3 %collective-permute-start.16 = (f32[32,4,128]{2,1,0:T(4,128)S(1)}, f32[32,4,128]{2,1,0:T(4,128)S(1)}, u32[]{:S(2)}, u32[]{:S(2)}) collective-permute-start(f32[32,4,128]{2,1,0:T(4,128)S(1)} %get-tuple-element.255), channel_id=1, source_target_pairs={{0,2},{1,3},{4,6},{5,7},{8,10},{9,11},{12,14},{13,15},{16,18},{17,... | collective-permute-start | bytes 196616 | tf_op jit(solution)/shard_map/ppermute | solution.py:25
  94.4 6.2 %collective-permute-start.17 = (f32[32,4,128]{2,1,0:T(4,128)S(1)}, f32[32,4,128]{2,1,0:T(4,128)S(1)}, u32[]{:S(2)}, u32[]{:S(2)}) collective-permute-start(f32[32,4,128]{2,1,0:T(4,128)S(1)} %get-tuple-element.254), channel_id=1, source_target_pairs={{2,0},{3,1},{6,4},{7,5},{10,8},{11,9},{14,12},{15,13},{18,16},{19,... | collective-permute-start | bytes 196616 | tf_op jit(solution)/shard_map/ppermute | solution.py:27
  100.8 4.2 %collective-permute-start.18 = (f32[32,16,4]{2,1,0:T(8,128)S(1)}, f32[32,16,4]{2,1,0:T(8,128)S(1)}, u32[]{:S(2)}, u32[]{:S(2)}) collective-permute-start(f32[32,16,4]{2,1,0:T(8,128)S(1)} %get-tuple-element.229), channel_id=1, source_target_pairs={{0,1},{2,3},{4,5},{6,7},{8,9},{10,11},{12,13},{14,15},{16,17},{18,... | collective-permute-start | bytes 24584 | tf_op jit(solution)/shard_map/ppermute | solution.py:25
  102.1 3.4 %collective-permute-start.19 = (f32[32,16,4]{2,1,0:T(8,128)S(1)}, f32[32,16,4]{2,1,0:T(8,128)S(1)}, u32[]{:S(2)}, u32[]{:S(2)}) collective-permute-start(f32[32,16,4]{2,1,0:T(8,128)S(1)} %get-tuple-element.228), channel_id=1, source_target_pairs={{1,0},{3,2},{5,4},{7,6},{9,8},{11,10},{13,12},{15,14},{17,16},{19,... | collective-permute-start | bytes 24584 | tf_op jit(solution)/shard_map/ppermute | solution.py:27
  111.4 3.7 %collective-permute-start.20 = (f32[32,4,128]{2,1,0:T(4,128)S(1)}, f32[32,4,128]{2,1,0:T(4,128)S(1)}, u32[]{:S(2)}, u32[]{:S(2)}) collective-permute-start(f32[32,4,128]{2,1,0:T(4,128)S(1)} %get-tuple-element.249), channel_id=1, source_target_pairs={{0,2},{1,3},{4,6},{5,7},{8,10},{9,11},{12,14},{13,15},{16,18},{17,... | collective-permute-start | bytes 196616 | tf_op jit(solution)/shard_map/ppermute | solution.py:25
  113.0 6.2 %collective-permute-start.21 = (f32[32,4,128]{2,1,0:T(4,128)S(1)}, f32[32,4,128]{2,1,0:T(4,128)S(1)}, u32[]{:S(2)}, u32[]{:S(2)}) collective-permute-start(f32[32,4,128]{2,1,0:T(4,128)S(1)} %get-tuple-element.248), channel_id=1, source_target_pairs={{2,0},{3,1},{6,4},{7,5},{10,8},{11,9},{14,12},{15,13},{18,16},{19,... | collective-permute-start | bytes 196616 | tf_op jit(solution)/shard_map/ppermute | solution.py:27
  119.4 5.0 %collective-permute-start.22 = (f32[32,16,4]{2,1,0:T(8,128)S(1)}, f32[32,16,4]{2,1,0:T(8,128)S(1)}, u32[]{:S(2)}, u32[]{:S(2)}) collective-permute-start(f32[32,16,4]{2,1,0:T(8,128)S(1)} %get-tuple-element.217), channel_id=1, source_target_pairs={{0,1},{2,3},{4,5},{6,7},{8,9},{10,11},{12,13},{14,15},{16,17},{18,... | collective-permute-start | bytes 24584 | tf_op jit(solution)/shard_map/ppermute | solution.py:25
  120.8 3.6 %collective-permute-start.23 = (f32[32,16,4]{2,1,0:T(8,128)S(1)}, f32[32,16,4]{2,1,0:T(8,128)S(1)}, u32[]{:S(2)}, u32[]{:S(2)}) collective-permute-start(f32[32,16,4]{2,1,0:T(8,128)S(1)} %get-tuple-element.216), channel_id=1, source_target_pairs={{1,0},{3,2},{5,4},{7,6},{9,8},{11,10},{13,12},{15,14},{17,16},{19,... | collective-permute-start | bytes 24584 | tf_op jit(solution)/shard_map/ppermute | solution.py:27
  125.9 3.8 %collective-permute-start.24 = (f32[32,4,128]{2,1,0:T(4,128)S(1)}, f32[32,4,128]{2,1,0:T(4,128)S(1)}, u32[]{:S(2)}, u32[]{:S(2)}) collective-permute-start(f32[32,4,128]{2,1,0:T(4,128)S(1)} %get-tuple-element.247), channel_id=1, source_target_pairs={{0,2},{1,3},{4,6},{5,7},{8,10},{9,11},{12,14},{13,15},{16,18},{17,... | collective-permute-start | bytes 196616 | tf_op jit(solution)/shard_map/ppermute | solution.py:25
  127.4 6.8 %collective-permute-start.25 = (f32[32,4,128]{2,1,0:T(4,128)S(1)}, f32[32,4,128]{2,1,0:T(4,128)S(1)}, u32[]{:S(2)}, u32[]{:S(2)}) collective-permute-start(f32[32,4,128]{2,1,0:T(4,128)S(1)} %get-tuple-element.246), channel_id=1, source_target_pairs={{2,0},{3,1},{6,4},{7,5},{10,8},{11,9},{14,12},{15,13},{18,16},{19,... | collective-permute-start | bytes 196616 | tf_op jit(solution)/shard_map/ppermute | solution.py:27
  134.4 7.9 %collective-permute-start.26 = (f32[32,16,4]{2,1,0:T(8,128)S(1)}, f32[32,16,4]{2,1,0:T(8,128)S(1)}, u32[]{:S(2)}, u32[]{:S(2)}) collective-permute-start(f32[32,16,4]{2,1,0:T(8,128)S(1)} %get-tuple-element.213), channel_id=1, source_target_pairs={{0,1},{2,3},{4,5},{6,7},{8,9},{10,11},{12,13},{14,15},{16,17},{18,... | collective-permute-start | bytes 24584 | tf_op jit(solution)/shard_map/ppermute | solution.py:25
  136.4 6.0 %collective-permute-start.27 = (f32[32,16,4]{2,1,0:T(8,128)S(1)}, f32[32,16,4]{2,1,0:T(8,128)S(1)}, u32[]{:S(2)}, u32[]{:S(2)}) collective-permute-start(f32[32,16,4]{2,1,0:T(8,128)S(1)} %get-tuple-element.212), channel_id=1, source_target_pairs={{1,0},{3,2},{5,4},{7,6},{9,8},{11,10},{13,12},{15,14},{17,16},{19,... | collective-permute-start | bytes 24584 | tf_op jit(solution)/shard_map/ppermute | solution.py:27
  143.8 8.7 %collective-permute-start.28 = (f32[32,4,128]{2,1,0:T(4,128)S(1)}, f32[32,4,128]{2,1,0:T(4,128)S(1)}, u32[]{:S(2)}, u32[]{:S(2)}) collective-permute-start(f32[32,4,128]{2,1,0:T(4,128)S(1)} %get-tuple-element.245), channel_id=1, source_target_pairs={{0,2},{1,3},{4,6},{5,7},{8,10},{9,11},{12,14},{13,15},{16,18},{17,... | collective-permute-start | bytes 196616 | tf_op jit(solution)/shard_map/ppermute | solution.py:25
  145.3 7.2 %collective-permute-start.29 = (f32[32,4,128]{2,1,0:T(4,128)S(1)}, f32[32,4,128]{2,1,0:T(4,128)S(1)}, u32[]{:S(2)}, u32[]{:S(2)}) collective-permute-start(f32[32,4,128]{2,1,0:T(4,128)S(1)} %get-tuple-element.244), channel_id=1, source_target_pairs={{2,0},{3,1},{6,4},{7,5},{10,8},{11,9},{14,12},{15,13},{18,16},{19,... | collective-permute-start | bytes 196616 | tf_op jit(solution)/shard_map/ppermute | solution.py:27
  146.6 9.9 %collective-permute-start.32 = (f32[32,4,128]{2,1,0:T(4,128)S(1)}, f32[32,4,128]{2,1,0:T(4,128)S(1)}, u32[]{:S(2)}, u32[]{:S(2)}) collective-permute-start(f32[32,4,128]{2,1,0:T(4,128)S(1)} %get-tuple-element.253), channel_id=1, source_target_pairs={{0,2},{1,3},{4,6},{5,7},{8,10},{9,11},{12,14},{13,15},{16,18},{17,... | collective-permute-start | bytes 196616 | tf_op jit(solution)/shard_map/ppermute | solution.py:25
  151.2 6.3 %collective-permute-start.33 = (f32[32,4,128]{2,1,0:T(4,128)S(1)}, f32[32,4,128]{2,1,0:T(4,128)S(1)}, u32[]{:S(2)}, u32[]{:S(2)}) collective-permute-start(f32[32,4,128]{2,1,0:T(4,128)S(1)} %get-tuple-element.252), channel_id=1, source_target_pairs={{2,0},{3,1},{6,4},{7,5},{10,8},{11,9},{14,12},{15,13},{18,16},{19,... | collective-permute-start | bytes 196616 | tf_op jit(solution)/shard_map/ppermute | solution.py:27
  152.7 4.9 %collective-permute-start.30 = (f32[32,16,4]{2,1,0:T(8,128)S(1)}, f32[32,16,4]{2,1,0:T(8,128)S(1)}, u32[]{:S(2)}, u32[]{:S(2)}) collective-permute-start(f32[32,16,4]{2,1,0:T(8,128)S(1)} %get-tuple-element.209), channel_id=1, source_target_pairs={{0,1},{2,3},{4,5},{6,7},{8,9},{10,11},{12,13},{14,15},{16,17},{18,... | collective-permute-start | bytes 24584 | tf_op jit(solution)/shard_map/ppermute | solution.py:25
  155.0 3.4 %collective-permute-start.31 = (f32[32,16,4]{2,1,0:T(8,128)S(1)}, f32[32,16,4]{2,1,0:T(8,128)S(1)}, u32[]{:S(2)}, u32[]{:S(2)}) collective-permute-start(f32[32,16,4]{2,1,0:T(8,128)S(1)} %get-tuple-element.208), channel_id=1, source_target_pairs={{1,0},{3,2},{5,4},{7,6},{9,8},{11,10},{13,12},{15,14},{17,16},{19,... | collective-permute-start | bytes 24584 | tf_op jit(solution)/shard_map/ppermute | solution.py:27
  160.8 5.9 %collective-permute-start.34 = (f32[32,16,4]{2,1,0:T(8,128)S(1)}, f32[32,16,4]{2,1,0:T(8,128)S(1)}, u32[]{:S(2)}, u32[]{:S(2)}) collective-permute-start(f32[32,16,4]{2,1,0:T(8,128)S(1)} %get-tuple-element.225), channel_id=1, source_target_pairs={{0,1},{2,3},{4,5},{6,7},{8,9},{10,11},{12,13},{14,15},{16,17},{18,... | collective-permute-start | bytes 24584 | tf_op jit(solution)/shard_map/ppermute | solution.py:25
  162.9 3.9 %collective-permute-start.35 = (f32[32,16,4]{2,1,0:T(8,128)S(1)}, f32[32,16,4]{2,1,0:T(8,128)S(1)}, u32[]{:S(2)}, u32[]{:S(2)}) collective-permute-start(f32[32,16,4]{2,1,0:T(8,128)S(1)} %get-tuple-element.224), channel_id=1, source_target_pairs={{1,0},{3,2},{5,4},{7,6},{9,8},{11,10},{13,12},{15,14},{17,16},{19,... | collective-permute-start | bytes 24584 | tf_op jit(solution)/shard_map/ppermute | solution.py:27
  200.0 7.4 %copy-start.2 = (f32[32,8,128]{2,1,0:T(8,128)S(1)}, f32[32,8,128]{2,1,0:T(8,128)}, u32[]{:S(2)}) copy-start(f32[32,8,128]{2,1,0:T(8,128)} %get-tuple-element.194) | copy-start | bytes 393220
  200.0 7.4 %copy-start.3 = (f32[32,8,128]{2,1,0:T(8,128)S(1)}, f32[32,8,128]{2,1,0:T(8,128)}, u32[]{:S(2)}) copy-start(f32[32,8,128]{2,1,0:T(8,128)} %get-tuple-element.195) | copy-start | bytes 393220
  208.1 7.6 %collective-permute-start.36 = (f32[32,4,128]{2,1,0:T(4,128)S(1)}, f32[32,4,128]{2,1,0:T(4,128)S(1)}, u32[]{:S(2)}, u32[]{:S(2)}) collective-permute-start(f32[32,4,128]{2,1,0:T(4,128)S(1)} %get-tuple-element.243), channel_id=1, source_target_pairs={{0,2},{1,3},{4,6},{5,7},{8,10},{9,11},{12,14},{13,15},{16,18},{17,... | collective-permute-start | bytes 196616 | tf_op jit(solution)/shard_map/ppermute | solution.py:25
  211.8 6.2 %collective-permute-start.37 = (f32[32,4,128]{2,1,0:T(4,128)S(1)}, f32[32,4,128]{2,1,0:T(4,128)S(1)}, u32[]{:S(2)}, u32[]{:S(2)}) collective-permute-start(f32[32,4,128]{2,1,0:T(4,128)S(1)} %get-tuple-element.242), channel_id=1, source_target_pairs={{2,0},{3,1},{6,4},{7,5},{10,8},{11,9},{14,12},{15,13},{18,16},{19,... | collective-permute-start | bytes 196616 | tf_op jit(solution)/shard_map/ppermute | solution.py:27
  218.1 3.2 %collective-permute-start.38 = (f32[32,16,4]{2,1,0:T(8,128)S(1)}, f32[32,16,4]{2,1,0:T(8,128)S(1)}, u32[]{:S(2)}, u32[]{:S(2)}) collective-permute-start(f32[32,16,4]{2,1,0:T(8,128)S(1)} %get-tuple-element.205), channel_id=1, source_target_pairs={{0,1},{2,3},{4,5},{6,7},{8,9},{10,11},{12,13},{14,15},{16,17},{18,... | collective-permute-start | bytes 24584 | tf_op jit(solution)/shard_map/ppermute | solution.py:25
  219.4 3.4 %collective-permute-start.39 = (f32[32,16,4]{2,1,0:T(8,128)S(1)}, f32[32,16,4]{2,1,0:T(8,128)S(1)}, u32[]{:S(2)}, u32[]{:S(2)}) collective-permute-start(f32[32,16,4]{2,1,0:T(8,128)S(1)} %get-tuple-element.204), channel_id=1, source_target_pairs={{1,0},{3,2},{5,4},{7,6},{9,8},{11,10},{13,12},{15,14},{17,16},{19,... | collective-permute-start | bytes 24584 | tf_op jit(solution)/shard_map/ppermute | solution.py:27
Sparse Core Ops, SparseCore 0:
  160.8 37.5 all-reduce.12
where the time goes:
time: 233 us; the launch traced here: 232 us
  starting transfers between devices  74 us (32%)
  waiting for transfers between devices  63 us (27%)
  other arithmetic  45.3 us (19%)
  blocking collectives  19.9 us (9%)
  between operations  19.5 us (8%)
  local copies, waits for them, and re-layouts  10.1 us (4%)
    ppermute x20, starting transfers between devices, padded_2(): lax.ppermute(tail, axis, [(i, (i + 1) % count) for i in range(ends)])  47.7 us
    psum x1, waiting for transfers between devices, shards(): grad_all, illum_all = lax.psum((grad, illum), 'shots')  31.3 us
    ppermute x20, waiting for transfers between devices, padded_2(): lax.ppermute(head, axis, [((i + 1) % count, i) for i in range(ends)])  29.7 us
    ppermute x20, starting transfers between devices, padded_2(): lax.ppermute(head, axis, [((i + 1) % count, i) for i in range(ends)])  26.2 us
    scatter-add x10, other arithmetic, place_local(): flat = jnp.zeros((rows * cols,), jnp.float32).at[spots].add(kept)  24.9 us
    all_gather x1, blocking collectives, shards(): full_vel = lax.all_gather(velocity, 'shots', axis=0, tiled=True)  13.6 us
    concatenate x30, other arithmetic, padded_2(): jnp.concatenate([lax.ppermute(tail, axis, [(i, (i + 1) % count) for i in...  8.09 us
    pmax x1, blocking collectives, shards(): peak = lax.pmax(jnp.max(jnp.abs(precond)), ('dom', 'sub'))  6.3 us
  transfers between devices with their start and end apart: 41, of which 16 were waited for; matrix products, arithmetic and copies ran while one was open for 14% of the time, Pallas kernels for 0%

commit v1 on v0

--- a/solution.py
+++ b/solution.py
@@ -12,6 +12,24 @@
 src_depth = 2
 rec_depth = 1
 reach = 4
+
+
+def in_order(blocks, dim):
+    shape = list(blocks.shape[1:])
+    shape[dim] *= blocks.shape[0]
+    return jnp.moveaxis(blocks, 0, dim).reshape(shape)
+
+
+def grow_blocks(shard, axis):
+    size = lax.axis_size(axis)
+    blocks = shard[None]
+    for level in range(size.bit_length() - 1):
+        bit = 1 << level
+        theirs = lax.ppermute(blocks, axis, [(i, i ^ bit) for i in range(size)])
+        both = jnp.stack([blocks, theirs])
+        upper = lax.axis_index(axis) >> level & 1
+        blocks = jnp.where(upper == 0, both, both[::-1]).reshape(-1, *shard.shape)
+    return blocks
 
 
 def padded_2(cells, sides, width):
@@ -75,7 +93,7 @@
     velocity, wave_prev, wave_now, adj_next, adj_now, sponge, wavelet, src_pos, rec_pos, observed
 ):
     depth, rows, cols = sponge.shape
-    full_vel = lax.all_gather(velocity, "shots", axis=0, tiled=True)
+    full_vel = in_order(grow_blocks(velocity, "shots"), 0)
     kappa = full_vel * full_vel
     damp = damp_rate * sponge.astype(jnp.float32)
     amps = wavelet[0]

time: 233 us -> 223 us (0.957)
  blocking collectives: 19.9 us -> 6.3 us
  starting transfers between devices: 74 us -> 77.8 us
    all_gather x1 -> x0, blocking collectives: 13.6 us -> none  [shards(): full_vel = lax.all_gather(velocity, 'shots', axis=0, tiled=True)]
    ppermute x0 -> x2, starting transfers between devices: none -> 4.3 us  [grow_blocks(): theirs = lax.ppermute(blocks, axis, [(i, i ^ bit) for i in range(size)])]
    psum x1, waiting for transfers between devices: 31.3 us -> 28.4 us  [shards(): grad_all, illum_all = lax.psum((grad, illum), 'shots')]
  transfers between devices with their start and end apart: 41 -> 43, of which waited for: 16 -> 17; matrix products, arithmetic and copies ran while one was open for 14% -> 15% of each run, Pallas kernels for 0% -> 0%
where the time goes in v1:
time: 223 us; the launch traced here: 221 us
  starting transfers between devices  77.8 us (35%)
  waiting for transfers between devices  61.7 us (28%)
  other arithmetic  45.5 us (20%)
  between operations  19.6 us (9%)
  local copies, waits for them, and re-layouts  10.5 us (5%)
  blocking collectives  6.3 us (3%)
    ppermute x20, starting transfers between devices, padded_2(): lax.ppermute(tail, axis, [(i, (i + 1) % count) for i in range(ends)])  47.2 us
    ppermute x20, waiting for transfers between devices, padded_2(): lax.ppermute(head, axis, [((i + 1) % count, i) for i in range(ends)])  31.4 us
    psum x1, waiting for transfers between devices, shards(): grad_all, illum_all = lax.psum((grad, illum), 'shots')  28.4 us
    ppermute x20, starting transfers between devices, padded_2(): lax.ppermute(head, axis, [((i + 1) % count, i) for i in range(ends)])  26.2 us
    scatter-add x10, other arithmetic, place_local(): flat = jnp.zeros((rows * cols,), jnp.float32).at[spots].add(kept)  25.2 us
    concatenate x30, other arithmetic, padded_2(): jnp.concatenate([lax.ppermute(tail, axis, [(i, (i + 1) % count) for i in...  8.08 us
    pmax x1, blocking collectives, shards(): peak = lax.pmax(jnp.max(jnp.abs(precond)), ('dom', 'sub'))  6.3 us
    add x10, other arithmetic, advance(): numer = 2.0 * now - (1.0 - damp) * before + kappa * lap  5.95 us
  transfers between devices with their start and end apart: 43, of which 17 were waited for; matrix products, arithmetic and copies ran while one was open for 15% of the time, Pallas kernels for 0%

profile of v1, /device:TPU:0, one launch (start us, length us, event | category | flops | bytes accessed | tf_op | source)
XLA Modules:
  0.0 221.4 jit_solution(8008560285924287874)
XLA Ops:
  8.1 4.9 %collective-permute-start.6 = (f32[32,4,128]{2,1,0:T(4,128)S(1)}, f32[32,4,128]{2,1,0:T(4,128)S(1)}, u32[]{:S(2)}, u32[]{:S(2)}) collective-permute-start(f32[32,4,128]{2,1,0:T(4,128)S(1)} %get-tuple-element.261), channel_id=1, source_target_pairs={{0,2},{1,3},{4,6},{5,7},{8,10},{9,11},{12,14},{13,15},{16,18},{17,... | collective-permute-start | bytes 196616 | tf_op jit(solution)/shard_map/ppermute | solution.py:43
  13.0 1.3 collective-permute-start.7
  14.3 1.6 collective-permute-start
  16.0 4.5 %collective-permute-start.2 = (f32[32,4,128]{2,1,0:T(4,128)S(1)}, f32[32,4,128]{2,1,0:T(4,128)S(1)}, u32[]{:S(2)}, u32[]{:S(2)}) collective-permute-start(f32[32,4,128]{2,1,0:T(4,128)S(1)} %get-tuple-element.251), channel_id=1, source_target_pairs={{0,2},{1,3},{4,6},{5,7},{8,10},{9,11},{12,14},{13,15},{16,18},{17,... | collective-permute-start | bytes 196616 | tf_op jit(solution)/shard_map/ppermute | solution.py:43
  20.6 1.3 collective-permute-start.3
  28.8 2.7 %fusion.347 = f32[1024]{0:T(1024)S(1)} fusion(f32[1024]{0:T(1024)S(1)} %broadcast.399.clone, s32[]{:T(128)} %bitcast.19, pred[1]{0:T(512)(128)(4,1)} %get-tuple-element.277, f32[1,1]{1,0:T(1,128)} %get-tuple-element.272, s32[1]{0:T(128)} %compare_select_fusion.1), kind=kLoop, calls=%fused_computation.693 | loop fusion | flops 5 | bytes 525 | tf_op jit(solution)/shard_map/scatter-add | solution.py:88
  31.6 2.6 %fusion.345 = f32[1024]{0:T(1024)S(1)} fusion(f32[1024]{0:T(1024)S(1)} %broadcast.399.clone.1, s32[]{:T(128)} %bitcast.19, pred[1]{0:T(512)(128)(4,1)} %get-tuple-element.277, f32[1,1]{1,0:T(1,128)} %get-tuple-element.271, s32[1]{0:T(128)} %compare_select_fusion.1), kind=kLoop, calls=%fused_computation.690 | loop fusion | flops 5 | bytes 525 | tf_op jit(solution)/shard_map/scatter-add | solution.py:88
  34.2 2.7 %fusion.343 = f32[1024]{0:T(1024)S(1)} fusion(f32[1024]{0:T(1024)S(1)} %broadcast.399.clone.2, s32[]{:T(128)} %bitcast.19, pred[1]{0:T(512)(128)(4,1)} %get-tuple-element.277, f32[1,1]{1,0:T(1,128)} %get-tuple-element.270, s32[1]{0:T(128)} %compare_select_fusion.1), kind=kLoop, calls=%fused_computation.687 | loop fusion | flops 5 | bytes 525 | tf_op jit(solution)/shard_map/scatter-add | solution.py:88
  36.9 2.6 %fusion.341 = f32[1024]{0:T(1024)S(1)} fusion(f32[1024]{0:T(1024)S(1)} %broadcast.399.clone.3, s32[]{:T(128)} %bitcast.19, pred[1]{0:T(512)(128)(4,1)} %get-tuple-element.277, f32[1,1]{1,0:T(1,128)} %get-tuple-element.269, s32[1]{0:T(128)} %compare_select_fusion.1), kind=kLoop, calls=%fused_computation.684 | loop fusion | flops 5 | bytes 525 | tf_op jit(solution)/shard_map/scatter-add | solution.py:88
  39.5 2.7 %collective-permute-start.1 = (f32[2,8,8,128]{3,2,1,0:T(8,128)S(1)}, f32[2,8,8,128]{3,2,1,0:T(8,128)S(1)}, u32[]{:S(2)}, u32[]{:S(2)}) collective-permute-start(f32[2,8,8,128]{3,2,1,0:T(8,128)S(1)} %get-tuple-element.263), channel_id=1, source_target_pairs={{0,8},{4,12},{8,0},{12,4},{1,9},{5,13},{9,1},{13,5},{2,10},{6,14},... | collective-permute-start | bytes 196616 | tf_op jit(solution)/shard_map/ppermute | solution.py:28
  42.4 1.3 collective-permute-start.8
  43.7 1.3 collective-permute-start.9
  45.2 3.1 %collective-permute-start.4 = (f32[32,16,4]{2,1,0:T(8,128)S(1)}, f32[32,16,4]{2,1,0:T(8,128)S(1)}, u32[]{:S(2)}, u32[]{:S(2)}) collective-permute-start(f32[32,16,4]{2,1,0:T(8,128)S(1)} %get-tuple-element.221), channel_id=1, source_target_pairs={{0,1},{2,3},{4,5},{6,7},{8,9},{10,11},{12,13},{14,15},{16,17},{18,... | collective-permute-start | bytes 24584 | tf_op jit(solution)/shard_map/ppermute | solution.py:43
  48.3 1.3 collective-permute-start.5
  50.0 1.7 collective-permute-done.5
  54.1 4.5 %collective-permute-start.10 = (f32[32,4,128]{2,1,0:T(4,128)S(1)}, f32[32,4,128]{2,1,0:T(4,128)S(1)}, u32[]{:S(2)}, u32[]{:S(2)}) collective-permute-start(f32[32,4,128]{2,1,0:T(4,128)S(1)} %get-tuple-element.259), channel_id=1, source_target_pairs={{0,2},{1,3},{4,6},{5,7},{8,10},{9,11},{12,14},{13,15},{16,18},{17,... | collective-permute-start | bytes 196616 | tf_op jit(solution)/shard_map/ppermute | solution.py:43
  58.7 1.3 collective-permute-start.11
  60.6 4.3 %collective-permute-done.11 = f32[32,4,128]{2,1,0:T(4,128)S(1)} collective-permute-done((f32[32,4,128]{2,1,0:T(4,128)S(1)}, f32[32,4,128]{2,1,0:T(4,128)S(1)}, u32[]{:S(2)}, u32[]{:S(2)}) %collective-permute-start.11) | collective-permute-done | bytes 65568 | tf_op jit(solution)/shard_map/ppermute | solution.py:45
  65.1 1.3 collective-permute-start.12
  66.4 1.3 collective-permute-start.13
  68.3 1.5 collective-permute-done.13
  71.3 1.6 collective-permute-start.14
  72.8 1.3 collective-permute-start.15
  74.2 1.4 gather_fusion.3
  75.5 3.5 %collective-permute-done.15 = f32[32,4,128]{2,1,0:T(4,128)S(1)} collective-permute-done((f32[32,4,128]{2,1,0:T(4,128)S(1)}, f32[32,4,128]{2,1,0:T(4,128)S(1)}, u32[]{:S(2)}, u32[]{:S(2)}) %collective-permute-start.15) | collective-permute-done | bytes 65568 | tf_op jit(solution)/shard_map/ppermute | solution.py:45
  79.2 1.3 collective-permute-start.16
  80.5 1.3 collective-permute-start.17
  81.8 2.1 collective-permute-done.17
  85.4 1.6 collective-permute-start.18
  87.0 1.3 collective-permute-start.19
  88.3 1.4 gather_fusion.2
  89.7 3.5 %collective-permute-done.19 = f32[32,4,128]{2,1,0:T(4,128)S(1)} collective-permute-done((f32[32,4,128]{2,1,0:T(4,128)S(1)}, f32[32,4,128]{2,1,0:T(4,128)S(1)}, u32[]{:S(2)}, u32[]{:S(2)}) %collective-permute-start.19) | collective-permute-done | bytes 65568 | tf_op jit(solution)/shard_map/ppermute | solution.py:45
  93.3 1.3 collective-permute-start.20
  94.6 1.5 collective-permute-start.21
  96.1 1.4 gather_fusion.1
  100.2 1.4 gather_fusion
  101.6 2.3 %scatter_custom_fusion = f32[1024]{0:T(1024)S(1)} fusion(s32[256]{0:T(256)S(1)} %bitcast.146, f32[256]{0:T(256)S(1)} %get-tuple-element.276, f32[]{:T(128)} %constant.410.clone.1), kind=kCustom, calls=%fused_computation.654 | custom fusion | flops 256 | bytes 4100 | tf_op jit(solution)/shard_map/scatter-add | solution.py:88
  104.0 1.6 collective-permute-start.22
  105.5 1.3 collective-permute-start.23
  107.6 4.1 %collective-permute-done.23 = f32[32,4,128]{2,1,0:T(4,128)S(1)} collective-permute-done((f32[32,4,128]{2,1,0:T(4,128)S(1)}, f32[32,4,128]{2,1,0:T(4,128)S(1)}, u32[]{:S(2)}, u32[]{:S(2)}) %collective-permute-start.23) | collective-permute-done | bytes 65568 | tf_op jit(solution)/shard_map/ppermute | solution.py:45
  111.9 1.4 collective-permute-start.24
  113.3 1.3 collective-permute-start.25
  114.6 2.3 %scatter_custom_fusion.1 = f32[1024]{0:T(1024)S(1)} fusion(s32[256]{0:T(256)S(1)} %bitcast.147, f32[256]{0:T(256)S(1)} %get-tuple-element.275, f32[]{:T(128)} %constant.410.clone.1), kind=kCustom, calls=%fused_computation.652 | custom fusion | flops 256 | bytes 4100 | tf_op jit(solution)/shard_map/scatter-add | solution.py:88
  118.4 1.5 collective-permute-start.26
  120.0 1.3 collective-permute-start.27
  122.2 4.5 %collective-permute-done.27 = f32[32,4,128]{2,1,0:T(4,128)S(1)} collective-permute-done((f32[32,4,128]{2,1,0:T(4,128)S(1)}, f32[32,4,128]{2,1,0:T(4,128)S(1)}, u32[]{:S(2)}, u32[]{:S(2)}) %collective-permute-start.27) | collective-permute-done | bytes 65568 | tf_op jit(solution)/shard_map/ppermute | solution.py:45
  126.9 2.0 collective-permute-start.28
  128.9 1.3 collective-permute-start.29
  130.2 2.3 %scatter_custom_fusion.3 = f32[1024]{0:T(1024)S(1)} fusion(s32[256]{0:T(256)S(1)} %bitcast.148, f32[256]{0:T(256)S(1)} %get-tuple-element.200, f32[]{:T(128)} %constant.410.clone.1), kind=kCustom, calls=%fused_computation.648 | custom fusion | flops 256 | bytes 4100 | tf_op jit(solution)/shard_map/scatter-add | solution.py:88
  132.5 2.3 %scatter_custom_fusion.2 = f32[1024]{0:T(1024)S(1)} fusion(s32[256]{0:T(256)S(1)} %bitcast.149, f32[256]{0:T(256)S(1)} %get-tuple-element.274, f32[]{:T(128)} %constant.410.clone.1), kind=kCustom, calls=%fused_computation.650 | custom fusion | flops 256 | bytes 4100 | tf_op jit(solution)/shard_map/scatter-add | solution.py:88
  136.3 1.5 collective-permute-start.30
  139.1 4.5 %collective-permute-start.34 = (f32[32,4,128]{2,1,0:T(4,128)S(1)}, f32[32,4,128]{2,1,0:T(4,128)S(1)}, u32[]{:S(2)}, u32[]{:S(2)}) collective-permute-start(f32[32,4,128]{2,1,0:T(4,128)S(1)} %get-tuple-element.253), channel_id=1, source_target_pairs={{0,2},{1,3},{4,6},{5,7},{8,10},{9,11},{12,14},{13,15},{16,18},{17,... | collective-permute-start | bytes 196616 | tf_op jit(solution)/shard_map/ppermute | solution.py:43
  145.2 2.3 %collective-permute-start.32 = (f32[32,16,4]{2,1,0:T(8,128)S(1)}, f32[32,16,4]{2,1,0:T(8,128)S(1)}, u32[]{:S(2)}, u32[]{:S(2)}) collective-permute-start(f32[32,16,4]{2,1,0:T(8,128)S(1)} %get-tuple-element.209), channel_id=1, source_target_pairs={{0,1},{2,3},{4,5},{6,7},{8,9},{10,11},{12,13},{14,15},{16,17},{18,... | collective-permute-start | bytes 24584 | tf_op jit(solution)/shard_map/ppermute | solution.py:43
  147.5 1.5 collective-permute-start.33
  153.3 2.1 collective-permute-start.36
  156.7 2.7 %fusion.339 = f32[1024]{0:T(1024)S(1)} fusion(f32[1024]{0:T(1024)S(1)} %broadcast.399.clone.4, s32[]{:T(128)} %bitcast.19, pred[1]{0:T(512)(128)(4,1)} %get-tuple-element.277, f32[1,1]{1,0:T(1,128)} %get-tuple-element.273, s32[1]{0:T(128)} %compare_select_fusion.1), kind=kLoop, calls=%fused_computation.681 | loop fusion | flops 5 | bytes 525 | tf_op jit(solution)/shard_map/scatter-add | solution.py:88
  159.7 28.4 %all-reduce.13.cloned.1.call-done = (f32[32,8,128]{2,1,0:T(8,128)}, f32[32,8,128]{2,1,0:T(8,128)}) async-done(((f32[32,8,128]{2,1,0:T(8,128)}, f32[32,8,128]{2,1,0:T(8,128)}), (f32[32,8,128]{2,1,0:T(8,128)}, f32[32,8,128]{2,1,0:T(8,128)})) %all-reduce.13.cloned.1.call-update) | async-done | bytes 262160 | tf_op jit(solution)/shard_map/psum | solution.py:122
  188.1 1.6 abs_reduce_fusion
  190.1 6.3 %pmax.7 = f32[]{:T(128)} all-reduce(f32[]{:T(128)} %abs_reduce_fusion), channel_id=1, replica_groups=mesh['groups'=2,'shots'=4,'dom'=2,'sub'=2] {'dom','sub'}, use_global_device_ids=true, to_apply=%region_7.8 | all-reduce | flops 1 | bytes 8 | tf_op jit(solution)/shard_map/pmax | solution.py:124
  197.7 3.6 %collective-permute-start.38 = (f32[32,4,128]{2,1,0:T(4,128)S(1)}, f32[32,4,128]{2,1,0:T(4,128)S(1)}, u32[]{:S(2)}, u32[]{:S(2)}) collective-permute-start(f32[32,4,128]{2,1,0:T(4,128)S(1)} %get-tuple-element.243), channel_id=1, source_target_pairs={{0,2},{1,3},{4,6},{5,7},{8,10},{9,11},{12,14},{13,15},{16,18},{17,... | collective-permute-start | bytes 196616 | tf_op jit(solution)/shard_map/ppermute | solution.py:43
  202.7 2.6 %fusion.337 = f32[1024]{0:T(1024)S(1)} fusion(f32[1024]{0:T(1024)S(1)} %broadcast.399.clone.5, s32[]{:T(128)} %bitcast.19, pred[1]{0:T(512)(128)(4,1)} %get-tuple-element.277, f32[1,1]{1,0:T(1,128)} %get-tuple-element.268, s32[1]{0:T(128)} %compare_select_fusion.1), kind=kLoop, calls=%fused_computation.678 | loop fusion | flops 5 | bytes 525 | tf_op jit(solution)/shard_map/scatter-add | solution.py:88
  205.3 2.3 %collective-permute-done.39 = f32[32,4,128]{2,1,0:T(4,128)S(1)} collective-permute-done((f32[32,4,128]{2,1,0:T(4,128)S(1)}, f32[32,4,128]{2,1,0:T(4,128)S(1)}, u32[]{:S(2)}, u32[]{:S(2)}) %collective-permute-start.39) | collective-permute-done | bytes 65568 | tf_op jit(solution)/shard_map/ppermute | solution.py:45
  207.7 1.3 collective-permute-start.40
  211.0 1.5 collective-permute-done.41
  (165 shorter events, 34.7 us)
Async XLA Ops:
  7.2 180.9 %all-reduce.13.cloned.1.call-start = ((), (), s32[]{:S(2)}) async-start(), calls=%async_computation | async-start | bytes 524288 | tf_op jit(solution)/shard_map/psum | solution.py:122
  8.1 6.2 %copy-start.7 = (f32[8,8,128]{2,1,0:T(8,128)S(1)}, f32[8,8,128]{2,1,0:T(8,128)}, u32[]{:S(2)}) copy-start(f32[8,8,128]{2,1,0:T(8,128)} %param.42) | copy-start | bytes 98308
  8.1 7.9 %copy-start.4 = (bf16[1,32,8,128]{3,2,1,0:T(8,128)(2,1)S(1)}, bf16[1,32,8,128]{3,2,1,0:T(8,128)(2,1)}, u32[]{:S(2)}) copy-start(bf16[1,32,8,128]{3,2,1,0:T(8,128)(2,1)} %param.46) | copy-start | bytes 196612
  8.1 34.1 %collective-permute-start.6 = (f32[32,4,128]{2,1,0:T(4,128)S(1)}, f32[32,4,128]{2,1,0:T(4,128)S(1)}, u32[]{:S(2)}, u32[]{:S(2)}) collective-permute-start(f32[32,4,128]{2,1,0:T(4,128)S(1)} %get-tuple-element.261), channel_id=1, source_target_pairs={{0,2},{1,3},{4,6},{5,7},{8,10},{9,11},{12,14},{13,15},{16,18},{17,... | collective-permute-start | bytes 196616 | tf_op jit(solution)/shard_map/ppermute | solution.py:43
  13.0 29.2 %collective-permute-start.7 = (f32[32,4,128]{2,1,0:T(4,128)S(1)}, f32[32,4,128]{2,1,0:T(4,128)S(1)}, u32[]{:S(2)}, u32[]{:S(2)}) collective-permute-start(f32[32,4,128]{2,1,0:T(4,128)S(1)} %get-tuple-element.260), channel_id=1, source_target_pairs={{2,0},{3,1},{6,4},{7,5},{10,8},{11,9},{14,12},{15,13},{18,16},{19,... | collective-permute-start | bytes 196616 | tf_op jit(solution)/shard_map/ppermute | solution.py:45
  14.3 25.2 %collective-permute-start = (f32[1,8,8,128]{3,2,1,0:T(8,128)S(1)}, f32[1,8,8,128]{3,2,1,0:T(8,128)S(1)}, u32[]{:S(2)}, u32[]{:S(2)}) collective-permute-start(f32[1,8,8,128]{3,2,1,0:T(8,128)S(1)} %bitcast.142), channel_id=1, source_target_pairs={{0,4},{4,0},{8,12},{12,8},{1,5},{5,1},{9,13},{13,9},{2,6},{6,2},{1... | collective-permute-start | bytes 98312 | tf_op jit(solution)/shard_map/ppermute | solution.py:28
  16.0 29.0 %collective-permute-start.2 = (f32[32,4,128]{2,1,0:T(4,128)S(1)}, f32[32,4,128]{2,1,0:T(4,128)S(1)}, u32[]{:S(2)}, u32[]{:S(2)}) collective-permute-start(f32[32,4,128]{2,1,0:T(4,128)S(1)} %get-tuple-element.251), channel_id=1, source_target_pairs={{0,2},{1,3},{4,6},{5,7},{8,10},{9,11},{12,14},{13,15},{16,18},{17,... | collective-permute-start | bytes 196616 | tf_op jit(solution)/shard_map/ppermute | solution.py:43
  20.6 24.5 %collective-permute-start.3 = (f32[32,4,128]{2,1,0:T(4,128)S(1)}, f32[32,4,128]{2,1,0:T(4,128)S(1)}, u32[]{:S(2)}, u32[]{:S(2)}) collective-permute-start(f32[32,4,128]{2,1,0:T(4,128)S(1)} %get-tuple-element.250), channel_id=1, source_target_pairs={{2,0},{3,1},{6,4},{7,5},{10,8},{11,9},{14,12},{15,13},{18,16},{19,... | collective-permute-start | bytes 196616 | tf_op jit(solution)/shard_map/ppermute | solution.py:45
  21.9 0.7 copy-start.8
  21.9 1.3 copy-start.9
  23.2 0.7 copy-start.10
  39.5 13.0 %collective-permute-start.1 = (f32[2,8,8,128]{3,2,1,0:T(8,128)S(1)}, f32[2,8,8,128]{3,2,1,0:T(8,128)S(1)}, u32[]{:S(2)}, u32[]{:S(2)}) collective-permute-start(f32[2,8,8,128]{3,2,1,0:T(8,128)S(1)} %get-tuple-element.263), channel_id=1, source_target_pairs={{0,8},{4,12},{8,0},{12,4},{1,9},{5,13},{9,1},{13,5},{2,10},{6,14},... | collective-permute-start | bytes 196616 | tf_op jit(solution)/shard_map/ppermute | solution.py:28
  42.4 7.2 %collective-permute-start.8 = (f32[32,16,4]{2,1,0:T(8,128)S(1)}, f32[32,16,4]{2,1,0:T(8,128)S(1)}, u32[]{:S(2)}, u32[]{:S(2)}) collective-permute-start(f32[32,16,4]{2,1,0:T(8,128)S(1)} %get-tuple-element.241), channel_id=1, source_target_pairs={{0,1},{2,3},{4,5},{6,7},{8,9},{10,11},{12,13},{14,15},{16,17},{18,... | collective-permute-start | bytes 24584 | tf_op jit(solution)/shard_map/ppermute | solution.py:43
  43.7 5.9 %collective-permute-start.9 = (f32[32,16,4]{2,1,0:T(8,128)S(1)}, f32[32,16,4]{2,1,0:T(8,128)S(1)}, u32[]{:S(2)}, u32[]{:S(2)}) collective-permute-start(f32[32,16,4]{2,1,0:T(8,128)S(1)} %get-tuple-element.240), channel_id=1, source_target_pairs={{1,0},{3,2},{5,4},{7,6},{9,8},{11,10},{13,12},{15,14},{17,16},{19,... | collective-permute-start | bytes 24584 | tf_op jit(solution)/shard_map/ppermute | solution.py:45
  45.2 4.7 %collective-permute-start.4 = (f32[32,16,4]{2,1,0:T(8,128)S(1)}, f32[32,16,4]{2,1,0:T(8,128)S(1)}, u32[]{:S(2)}, u32[]{:S(2)}) collective-permute-start(f32[32,16,4]{2,1,0:T(8,128)S(1)} %get-tuple-element.221), channel_id=1, source_target_pairs={{0,1},{2,3},{4,5},{6,7},{8,9},{10,11},{12,13},{14,15},{16,17},{18,... | collective-permute-start | bytes 24584 | tf_op jit(solution)/shard_map/ppermute | solution.py:43
  48.3 3.4 %collective-permute-start.5 = (f32[32,16,4]{2,1,0:T(8,128)S(1)}, f32[32,16,4]{2,1,0:T(8,128)S(1)}, u32[]{:S(2)}, u32[]{:S(2)}) collective-permute-start(f32[32,16,4]{2,1,0:T(8,128)S(1)} %get-tuple-element.220), channel_id=1, source_target_pairs={{1,0},{3,2},{5,4},{7,6},{9,8},{11,10},{13,12},{15,14},{17,16},{19,... | collective-permute-start | bytes 24584 | tf_op jit(solution)/shard_map/ppermute | solution.py:45
  52.5 0.9 copy-start
  52.5 0.9 copy-start.1
  52.5 0.9 copy-start.5
  54.1 6.4 %collective-permute-start.10 = (f32[32,4,128]{2,1,0:T(4,128)S(1)}, f32[32,4,128]{2,1,0:T(4,128)S(1)}, u32[]{:S(2)}, u32[]{:S(2)}) collective-permute-start(f32[32,4,128]{2,1,0:T(4,128)S(1)} %get-tuple-element.259), channel_id=1, source_target_pairs={{0,2},{1,3},{4,6},{5,7},{8,10},{9,11},{12,14},{13,15},{16,18},{17,... | collective-permute-start | bytes 196616 | tf_op jit(solution)/shard_map/ppermute | solution.py:43
  58.7 6.2 %collective-permute-start.11 = (f32[32,4,128]{2,1,0:T(4,128)S(1)}, f32[32,4,128]{2,1,0:T(4,128)S(1)}, u32[]{:S(2)}, u32[]{:S(2)}) collective-permute-start(f32[32,4,128]{2,1,0:T(4,128)S(1)} %get-tuple-element.258), channel_id=1, source_target_pairs={{2,0},{3,1},{6,4},{7,5},{10,8},{11,9},{14,12},{15,13},{18,16},{19,... | collective-permute-start | bytes 196616 | tf_op jit(solution)/shard_map/ppermute | solution.py:45
  64.9 2.8 %copy-start.6 = (bf16[1,32,8,128]{3,2,1,0:T(8,128)(2,1)S(1)}, bf16[1,32,8,128]{3,2,1,0:T(8,128)(2,1)}, u32[]{:S(2)}) copy-start(bf16[1,32,8,128]{3,2,1,0:T(8,128)(2,1)} %param.45) | copy-start | bytes 196612
  65.1 3.2 %collective-permute-start.12 = (f32[32,16,4]{2,1,0:T(8,128)S(1)}, f32[32,16,4]{2,1,0:T(8,128)S(1)}, u32[]{:S(2)}, u32[]{:S(2)}) collective-permute-start(f32[32,16,4]{2,1,0:T(8,128)S(1)} %get-tuple-element.237), channel_id=1, source_target_pairs={{0,1},{2,3},{4,5},{6,7},{8,9},{10,11},{12,13},{14,15},{16,17},{18,... | collective-permute-start | bytes 24584 | tf_op jit(solution)/shard_map/ppermute | solution.py:43
  66.4 3.4 %collective-permute-start.13 = (f32[32,16,4]{2,1,0:T(8,128)S(1)}, f32[32,16,4]{2,1,0:T(8,128)S(1)}, u32[]{:S(2)}, u32[]{:S(2)}) collective-permute-start(f32[32,16,4]{2,1,0:T(8,128)S(1)} %get-tuple-element.236), channel_id=1, source_target_pairs={{1,0},{3,2},{5,4},{7,6},{9,8},{11,10},{13,12},{15,14},{17,16},{19,... | collective-permute-start | bytes 24584 | tf_op jit(solution)/shard_map/ppermute | solution.py:45
  71.3 4.3 %collective-permute-start.14 = (f32[32,4,128]{2,1,0:T(4,128)S(1)}, f32[32,4,128]{2,1,0:T(4,128)S(1)}, u32[]{:S(2)}, u32[]{:S(2)}) collective-permute-start(f32[32,4,128]{2,1,0:T(4,128)S(1)} %get-tuple-element.257), channel_id=1, source_target_pairs={{0,2},{1,3},{4,6},{5,7},{8,10},{9,11},{12,14},{13,15},{16,18},{17,... | collective-permute-start | bytes 196616 | tf_op jit(solution)/shard_map/ppermute | solution.py:43
  72.8 6.2 %collective-permute-start.15 = (f32[32,4,128]{2,1,0:T(4,128)S(1)}, f32[32,4,128]{2,1,0:T(4,128)S(1)}, u32[]{:S(2)}, u32[]{:S(2)}) collective-permute-start(f32[32,4,128]{2,1,0:T(4,128)S(1)} %get-tuple-element.256), channel_id=1, source_target_pairs={{2,0},{3,1},{6,4},{7,5},{10,8},{11,9},{14,12},{15,13},{18,16},{19,... | collective-permute-start | bytes 196616 | tf_op jit(solution)/shard_map/ppermute | solution.py:45
  79.2 2.6 %collective-permute-start.16 = (f32[32,16,4]{2,1,0:T(8,128)S(1)}, f32[32,16,4]{2,1,0:T(8,128)S(1)}, u32[]{:S(2)}, u32[]{:S(2)}) collective-permute-start(f32[32,16,4]{2,1,0:T(8,128)S(1)} %get-tuple-element.233), channel_id=1, source_target_pairs={{0,1},{2,3},{4,5},{6,7},{8,9},{10,11},{12,13},{14,15},{16,17},{18,... | collective-permute-start | bytes 24584 | tf_op jit(solution)/shard_map/ppermute | solution.py:43
  80.5 3.4 %collective-permute-start.17 = (f32[32,16,4]{2,1,0:T(8,128)S(1)}, f32[32,16,4]{2,1,0:T(8,128)S(1)}, u32[]{:S(2)}, u32[]{:S(2)}) collective-permute-start(f32[32,16,4]{2,1,0:T(8,128)S(1)} %get-tuple-element.232), channel_id=1, source_target_pairs={{1,0},{3,2},{5,4},{7,6},{9,8},{11,10},{13,12},{15,14},{17,16},{19,... | collective-permute-start | bytes 24584 | tf_op jit(solution)/shard_map/ppermute | solution.py:45
  85.4 4.3 %collective-permute-start.18 = (f32[32,4,128]{2,1,0:T(4,128)S(1)}, f32[32,4,128]{2,1,0:T(4,128)S(1)}, u32[]{:S(2)}, u32[]{:S(2)}) collective-permute-start(f32[32,4,128]{2,1,0:T(4,128)S(1)} %get-tuple-element.255), channel_id=1, source_target_pairs={{0,2},{1,3},{4,6},{5,7},{8,10},{9,11},{12,14},{13,15},{16,18},{17,... | collective-permute-start | bytes 196616 | tf_op jit(solution)/shard_map/ppermute | solution.py:43
  87.0 6.2 %collective-permute-start.19 = (f32[32,4,128]{2,1,0:T(4,128)S(1)}, f32[32,4,128]{2,1,0:T(4,128)S(1)}, u32[]{:S(2)}, u32[]{:S(2)}) collective-permute-start(f32[32,4,128]{2,1,0:T(4,128)S(1)} %get-tuple-element.254), channel_id=1, source_target_pairs={{2,0},{3,1},{6,4},{7,5},{10,8},{11,9},{14,12},{15,13},{18,16},{19,... | collective-permute-start | bytes 196616 | tf_op jit(solution)/shard_map/ppermute | solution.py:45
  93.3 4.2 %collective-permute-start.20 = (f32[32,16,4]{2,1,0:T(8,128)S(1)}, f32[32,16,4]{2,1,0:T(8,128)S(1)}, u32[]{:S(2)}, u32[]{:S(2)}) collective-permute-start(f32[32,16,4]{2,1,0:T(8,128)S(1)} %get-tuple-element.229), channel_id=1, source_target_pairs={{0,1},{2,3},{4,5},{6,7},{8,9},{10,11},{12,13},{14,15},{16,17},{18,... | collective-permute-start | bytes 24584 | tf_op jit(solution)/shard_map/ppermute | solution.py:43
  94.6 3.4 %collective-permute-start.21 = (f32[32,16,4]{2,1,0:T(8,128)S(1)}, f32[32,16,4]{2,1,0:T(8,128)S(1)}, u32[]{:S(2)}, u32[]{:S(2)}) collective-permute-start(f32[32,16,4]{2,1,0:T(8,128)S(1)} %get-tuple-element.228), channel_id=1, source_target_pairs={{1,0},{3,2},{5,4},{7,6},{9,8},{11,10},{13,12},{15,14},{17,16},{19,... | collective-permute-start | bytes 24584 | tf_op jit(solution)/shard_map/ppermute | solution.py:45
  104.0 3.7 %collective-permute-start.22 = (f32[32,4,128]{2,1,0:T(4,128)S(1)}, f32[32,4,128]{2,1,0:T(4,128)S(1)}, u32[]{:S(2)}, u32[]{:S(2)}) collective-permute-start(f32[32,4,128]{2,1,0:T(4,128)S(1)} %get-tuple-element.249), channel_id=1, source_target_pairs={{0,2},{1,3},{4,6},{5,7},{8,10},{9,11},{12,14},{13,15},{16,18},{17,... | collective-permute-start | bytes 196616 | tf_op jit(solution)/shard_map/ppermute | solution.py:43
  105.5 6.2 %collective-permute-start.23 = (f32[32,4,128]{2,1,0:T(4,128)S(1)}, f32[32,4,128]{2,1,0:T(4,128)S(1)}, u32[]{:S(2)}, u32[]{:S(2)}) collective-permute-start(f32[32,4,128]{2,1,0:T(4,128)S(1)} %get-tuple-element.248), channel_id=1, source_target_pairs={{2,0},{3,1},{6,4},{7,5},{10,8},{11,9},{14,12},{15,13},{18,16},{19,... | collective-permute-start | bytes 196616 | tf_op jit(solution)/shard_map/ppermute | solution.py:45
  111.9 5.0 %collective-permute-start.24 = (f32[32,16,4]{2,1,0:T(8,128)S(1)}, f32[32,16,4]{2,1,0:T(8,128)S(1)}, u32[]{:S(2)}, u32[]{:S(2)}) collective-permute-start(f32[32,16,4]{2,1,0:T(8,128)S(1)} %get-tuple-element.217), channel_id=1, source_target_pairs={{0,1},{2,3},{4,5},{6,7},{8,9},{10,11},{12,13},{14,15},{16,17},{18,... | collective-permute-start | bytes 24584 | tf_op jit(solution)/shard_map/ppermute | solution.py:43
  113.3 3.6 %collective-permute-start.25 = (f32[32,16,4]{2,1,0:T(8,128)S(1)}, f32[32,16,4]{2,1,0:T(8,128)S(1)}, u32[]{:S(2)}, u32[]{:S(2)}) collective-permute-start(f32[32,16,4]{2,1,0:T(8,128)S(1)} %get-tuple-element.216), channel_id=1, source_target_pairs={{1,0},{3,2},{5,4},{7,6},{9,8},{11,10},{13,12},{15,14},{17,16},{19,... | collective-permute-start | bytes 24584 | tf_op jit(solution)/shard_map/ppermute | solution.py:45
  118.4 3.8 %collective-permute-start.26 = (f32[32,4,128]{2,1,0:T(4,128)S(1)}, f32[32,4,128]{2,1,0:T(4,128)S(1)}, u32[]{:S(2)}, u32[]{:S(2)}) collective-permute-start(f32[32,4,128]{2,1,0:T(4,128)S(1)} %get-tuple-element.247), channel_id=1, source_target_pairs={{0,2},{1,3},{4,6},{5,7},{8,10},{9,11},{12,14},{13,15},{16,18},{17,... | collective-permute-start | bytes 196616 | tf_op jit(solution)/shard_map/ppermute | solution.py:43
  120.0 6.8 %collective-permute-start.27 = (f32[32,4,128]{2,1,0:T(4,128)S(1)}, f32[32,4,128]{2,1,0:T(4,128)S(1)}, u32[]{:S(2)}, u32[]{:S(2)}) collective-permute-start(f32[32,4,128]{2,1,0:T(4,128)S(1)} %get-tuple-element.246), channel_id=1, source_target_pairs={{2,0},{3,1},{6,4},{7,5},{10,8},{11,9},{14,12},{15,13},{18,16},{19,... | collective-permute-start | bytes 196616 | tf_op jit(solution)/shard_map/ppermute | solution.py:45
  126.9 7.9 %collective-permute-start.28 = (f32[32,16,4]{2,1,0:T(8,128)S(1)}, f32[32,16,4]{2,1,0:T(8,128)S(1)}, u32[]{:S(2)}, u32[]{:S(2)}) collective-permute-start(f32[32,16,4]{2,1,0:T(8,128)S(1)} %get-tuple-element.213), channel_id=1, source_target_pairs={{0,1},{2,3},{4,5},{6,7},{8,9},{10,11},{12,13},{14,15},{16,17},{18,... | collective-permute-start | bytes 24584 | tf_op jit(solution)/shard_map/ppermute | solution.py:43
  128.9 6.0 %collective-permute-start.29 = (f32[32,16,4]{2,1,0:T(8,128)S(1)}, f32[32,16,4]{2,1,0:T(8,128)S(1)}, u32[]{:S(2)}, u32[]{:S(2)}) collective-permute-start(f32[32,16,4]{2,1,0:T(8,128)S(1)} %get-tuple-element.212), channel_id=1, source_target_pairs={{1,0},{3,2},{5,4},{7,6},{9,8},{11,10},{13,12},{15,14},{17,16},{19,... | collective-permute-start | bytes 24584 | tf_op jit(solution)/shard_map/ppermute | solution.py:45
  136.3 8.7 %collective-permute-start.30 = (f32[32,4,128]{2,1,0:T(4,128)S(1)}, f32[32,4,128]{2,1,0:T(4,128)S(1)}, u32[]{:S(2)}, u32[]{:S(2)}) collective-permute-start(f32[32,4,128]{2,1,0:T(4,128)S(1)} %get-tuple-element.245), channel_id=1, source_target_pairs={{0,2},{1,3},{4,6},{5,7},{8,10},{9,11},{12,14},{13,15},{16,18},{17,... | collective-permute-start | bytes 196616 | tf_op jit(solution)/shard_map/ppermute | solution.py:43
  137.8 7.2 %collective-permute-start.31 = (f32[32,4,128]{2,1,0:T(4,128)S(1)}, f32[32,4,128]{2,1,0:T(4,128)S(1)}, u32[]{:S(2)}, u32[]{:S(2)}) collective-permute-start(f32[32,4,128]{2,1,0:T(4,128)S(1)} %get-tuple-element.244), channel_id=1, source_target_pairs={{2,0},{3,1},{6,4},{7,5},{10,8},{11,9},{14,12},{15,13},{18,16},{19,... | collective-permute-start | bytes 196616 | tf_op jit(solution)/shard_map/ppermute | solution.py:45
  139.1 9.9 %collective-permute-start.34 = (f32[32,4,128]{2,1,0:T(4,128)S(1)}, f32[32,4,128]{2,1,0:T(4,128)S(1)}, u32[]{:S(2)}, u32[]{:S(2)}) collective-permute-start(f32[32,4,128]{2,1,0:T(4,128)S(1)} %get-tuple-element.253), channel_id=1, source_target_pairs={{0,2},{1,3},{4,6},{5,7},{8,10},{9,11},{12,14},{13,15},{16,18},{17,... | collective-permute-start | bytes 196616 | tf_op jit(solution)/shard_map/ppermute | solution.py:43
  143.7 6.3 %collective-permute-start.35 = (f32[32,4,128]{2,1,0:T(4,128)S(1)}, f32[32,4,128]{2,1,0:T(4,128)S(1)}, u32[]{:S(2)}, u32[]{:S(2)}) collective-permute-start(f32[32,4,128]{2,1,0:T(4,128)S(1)} %get-tuple-element.252), channel_id=1, source_target_pairs={{2,0},{3,1},{6,4},{7,5},{10,8},{11,9},{14,12},{15,13},{18,16},{19,... | collective-permute-start | bytes 196616 | tf_op jit(solution)/shard_map/ppermute | solution.py:45
  145.2 4.9 %collective-permute-start.32 = (f32[32,16,4]{2,1,0:T(8,128)S(1)}, f32[32,16,4]{2,1,0:T(8,128)S(1)}, u32[]{:S(2)}, u32[]{:S(2)}) collective-permute-start(f32[32,16,4]{2,1,0:T(8,128)S(1)} %get-tuple-element.209), channel_id=1, source_target_pairs={{0,1},{2,3},{4,5},{6,7},{8,9},{10,11},{12,13},{14,15},{16,17},{18,... | collective-permute-start | bytes 24584 | tf_op jit(solution)/shard_map/ppermute | solution.py:43
  147.5 3.4 %collective-permute-start.33 = (f32[32,16,4]{2,1,0:T(8,128)S(1)}, f32[32,16,4]{2,1,0:T(8,128)S(1)}, u32[]{:S(2)}, u32[]{:S(2)}) collective-permute-start(f32[32,16,4]{2,1,0:T(8,128)S(1)} %get-tuple-element.208), channel_id=1, source_target_pairs={{1,0},{3,2},{5,4},{7,6},{9,8},{11,10},{13,12},{15,14},{17,16},{19,... | collective-permute-start | bytes 24584 | tf_op jit(solution)/shard_map/ppermute | solution.py:45
  153.3 6.0 %collective-permute-start.36 = (f32[32,16,4]{2,1,0:T(8,128)S(1)}, f32[32,16,4]{2,1,0:T(8,128)S(1)}, u32[]{:S(2)}, u32[]{:S(2)}) collective-permute-start(f32[32,16,4]{2,1,0:T(8,128)S(1)} %get-tuple-element.225), channel_id=1, source_target_pairs={{0,1},{2,3},{4,5},{6,7},{8,9},{10,11},{12,13},{14,15},{16,17},{18,... | collective-permute-start | bytes 24584 | tf_op jit(solution)/shard_map/ppermute | solution.py:43
  155.4 4.0 %collective-permute-start.37 = (f32[32,16,4]{2,1,0:T(8,128)S(1)}, f32[32,16,4]{2,1,0:T(8,128)S(1)}, u32[]{:S(2)}, u32[]{:S(2)}) collective-permute-start(f32[32,16,4]{2,1,0:T(8,128)S(1)} %get-tuple-element.224), channel_id=1, source_target_pairs={{1,0},{3,2},{5,4},{7,6},{9,8},{11,10},{13,12},{15,14},{17,16},{19,... | collective-permute-start | bytes 24584 | tf_op jit(solution)/shard_map/ppermute | solution.py:45
  189.7 7.4 %copy-start.2 = (f32[32,8,128]{2,1,0:T(8,128)S(1)}, f32[32,8,128]{2,1,0:T(8,128)}, u32[]{:S(2)}) copy-start(f32[32,8,128]{2,1,0:T(8,128)} %get-tuple-element.194) | copy-start | bytes 393220
  189.7 7.4 %copy-start.3 = (f32[32,8,128]{2,1,0:T(8,128)S(1)}, f32[32,8,128]{2,1,0:T(8,128)}, u32[]{:S(2)}) copy-start(f32[32,8,128]{2,1,0:T(8,128)} %get-tuple-element.195) | copy-start | bytes 393220
  197.7 7.5 %collective-permute-start.38 = (f32[32,4,128]{2,1,0:T(4,128)S(1)}, f32[32,4,128]{2,1,0:T(4,128)S(1)}, u32[]{:S(2)}, u32[]{:S(2)}) collective-permute-start(f32[32,4,128]{2,1,0:T(4,128)S(1)} %get-tuple-element.243), channel_id=1, source_target_pairs={{0,2},{1,3},{4,6},{5,7},{8,10},{9,11},{12,14},{13,15},{16,18},{17,... | collective-permute-start | bytes 196616 | tf_op jit(solution)/shard_map/ppermute | solution.py:43
  201.4 6.2 %collective-permute-start.39 = (f32[32,4,128]{2,1,0:T(4,128)S(1)}, f32[32,4,128]{2,1,0:T(4,128)S(1)}, u32[]{:S(2)}, u32[]{:S(2)}) collective-permute-start(f32[32,4,128]{2,1,0:T(4,128)S(1)} %get-tuple-element.242), channel_id=1, source_target_pairs={{2,0},{3,1},{6,4},{7,5},{10,8},{11,9},{14,12},{15,13},{18,16},{19,... | collective-permute-start | bytes 196616 | tf_op jit(solution)/shard_map/ppermute | solution.py:45
  207.7 3.2 %collective-permute-start.40 = (f32[32,16,4]{2,1,0:T(8,128)S(1)}, f32[32,16,4]{2,1,0:T(8,128)S(1)}, u32[]{:S(2)}, u32[]{:S(2)}) collective-permute-start(f32[32,16,4]{2,1,0:T(8,128)S(1)} %get-tuple-element.205), channel_id=1, source_target_pairs={{0,1},{2,3},{4,5},{6,7},{8,9},{10,11},{12,13},{14,15},{16,17},{18,... | collective-permute-start | bytes 24584 | tf_op jit(solution)/shard_map/ppermute | solution.py:43
  209.1 3.4 %collective-permute-start.41 = (f32[32,16,4]{2,1,0:T(8,128)S(1)}, f32[32,16,4]{2,1,0:T(8,128)S(1)}, u32[]{:S(2)}, u32[]{:S(2)}) collective-permute-start(f32[32,16,4]{2,1,0:T(8,128)S(1)} %get-tuple-element.204), channel_id=1, source_target_pairs={{1,0},{3,2},{5,4},{7,6},{9,8},{11,10},{13,12},{15,14},{17,16},{19,... | collective-permute-start | bytes 24584 | tf_op jit(solution)/shard_map/ppermute | solution.py:45
Sparse Core Ops, SparseCore 0:
  153.3 34.7 all-reduce.12
